TPU v7x, 256 devices: a whole 4x4x8 slice. The times are simulated.
256 devices in a mesh: expert: 4 (over z_lo), dp: 64 (over y, x, z_hi, core).
Axes of the slice: x: 4, y: 4, z: 8 (z_hi: 2, z_lo: 4; z = z_hi * 4 + z_lo), core: 2. Of those that a mesh axis runs over, the one named last changes fastest.
Arguments:
- act_attn: bfloat16 [65536, 256], P(('expert', 'dp')), may hold values from -10 to 10
- dy_attn: bfloat16 [65536, 6144], P(('expert', 'dp')), may hold values from -10 to 10
- act_exp: bfloat16 [4, 8192, 128], P('expert', 'dp'), may hold values from -10 to 10
- dy_exp: bfloat16 [4, 8192, 6144], P('expert', 'dp'), may hold values from -10 to 10
- w_attn: float32 [256, 6144], P(('expert', 'dp')), may hold values from -0.3 to 0.3
- m_attn: float32 [256, 6144], P(('expert', 'dp')), may hold values from -1.5 to 1.5
- v_attn: float32 [256, 6144], P(('expert', 'dp')), may hold values from 0.05 to 1
- w_exp: float32 [4, 128, 6144], P('expert', 'dp'), may hold values from -0.3 to 0.3
- m_exp: float32 [4, 128, 6144], P('expert', 'dp'), may hold values from -1.5 to 1.5
- v_exp: float32 [4, 128, 6144], P('expert', 'dp'), may hold values from 0.05 to 1
Outputs:
- w_attn_new: float32 [256, 6144], P(('expert', 'dp'))
- m_attn_new: float32 [256, 6144], P(('expert', 'dp'))
- v_attn_new: float32 [256, 6144], P(('expert', 'dp'))
- w_exp_new: float32 [4, 128, 6144], P('expert', 'dp')
- m_exp_new: float32 [4, 128, 6144], P('expert', 'dp')
- v_exp_new: float32 [4, 128, 6144], P('expert', 'dp')
- attn_weights: bfloat16 [256, 6144], replicated
- expert_weights: bfloat16 [4, 128, 6144], P('expert')
All inputs are finite; a program needn't handle non-finite values.
Results may differ from a plain program's by a relative error of at most 0.0075.
Values may be sent and summed in bfloat16 or wider, within the bound.
A program may use at most 64 MiB of HBM per device.

v0:
```python
import math

import jax
import jax.numpy as jnp
from jax import lax
from jax.sharding import PartitionSpec as P

beta_first = 0.9
beta_second = 0.95
bias_first = 1.0 - 0.9**10
bias_second = 1.0 - 0.95**10
learn_rate = 0.01
decay_rate = 0.1
adam_eps = 1e-08


def contract_rows(left, right):
    return lax.dot_general(
        left, right, (((0,), (0,)), ((), ())), preferred_element_type=jnp.float32
    )


def adamw(grad, weight, moment, second, factor):
    scaled = factor * grad
    moment_new = beta_first * moment + (1.0 - beta_first) * scaled
    second_new = beta_second * second + (1.0 - beta_second) * scaled * scaled
    update = moment_new / bias_first / (jnp.sqrt(second_new / bias_second) + adam_eps)
    weight_new = weight - learn_rate * (update + decay_rate * weight)
    return (weight_new, moment_new, second_new)


def body(act_attn, dy_attn, act_exp, dy_exp, w_attn, m_attn, v_attn, w_exp, m_exp, v_exp):
    width = w_attn.shape[1]
    n_expert = lax.axis_size("expert")
    total_params = width * (act_attn.shape[1] + n_expert * act_exp.shape[2])
    limit = 0.5 * math.sqrt(total_params)
    g_attn = lax.psum_scatter(
        contract_rows(act_attn, dy_attn), ("expert", "dp"), scatter_dimension=0, tiled=True
    )
    sq_attn = jnp.sum(g_attn * g_attn)
    local_act = act_exp[0]
    local_dy = dy_exp[0]
    g_exp = lax.psum_scatter(
        contract_rows(local_act, local_dy), "dp", scatter_dimension=0, tiled=True
    )
    sq_exp = jnp.sum(g_exp * g_exp)
    summed = lax.psum((sq_attn, sq_exp), ("expert", "dp"))
    total = summed[0] + summed[1]
    norm = jnp.sqrt(total)
    factor = jnp.minimum(1.0, limit / (norm + 1e-06))
    wa_new, ma_new, va_new = adamw(g_attn, w_attn, m_attn, v_attn, factor)
    we_new, me_new, ve_new = adamw(g_exp[None], w_exp, m_exp, v_exp, factor)
    attn_half = wa_new.astype(jnp.bfloat16)
    attn_full = lax.all_gather(attn_half, ("expert", "dp"), axis=0, tiled=True)
    expert_full = lax.all_gather(we_new.astype(jnp.bfloat16), "dp", axis=1, tiled=True)
    return (wa_new, ma_new, va_new, we_new, me_new, ve_new, attn_full, expert_full)


def solution(mesh):
    return jax.shard_map(
        body,
        mesh=mesh,
        in_specs=(
            P(("expert", "dp"), None),
            P(("expert", "dp"), None),
            P("expert", "dp", None),
            P("expert", "dp", None),
            P(("expert", "dp"), None),
            P(("expert", "dp"), None),
            P(("expert", "dp"), None),
            P("expert", "dp", None),
            P("expert", "dp", None),
            P("expert", "dp", None),
        ),
        out_specs=(
            P(("expert", "dp"), None),
            P(("expert", "dp"), None),
            P(("expert", "dp"), None),
            P("expert", "dp", None),
            P("expert", "dp", None),
            P("expert", "dp", None),
            P(),
            P("expert", None, None),
        ),
        check_vma=False,
    )
```

profile of v0, /device:TPU:1, one launch (start us, length us, event | category | flops | bytes accessed | tf_op | source)
XLA Modules:
  0.0 1681.6 jit_solution(16280890841784815197)
XLA Ops:
  7.2 0.0 copy-start
  7.2 0.0 all-reduce.5.cloned.1.call-start
  7.2 1.8 copy-done
  9.1 4.5 fusion.9
  13.6 0.0 copy-start.4
  13.6 0.0 all-reduce.5.cloned.1.call-update
  13.6 0.0 copy-start.8
  13.6 0.0 copy-start.1
  13.7 0.0 copy-start.2
  13.7 0.0 copy-start.3
  13.7 0.0 copy-start.5
  13.7 0.0 copy-start.6
  13.7 0.0 copy-start.7
  13.7 0.0 all-reduce.7.cloned.1.call-start
  13.8 0.6 copy-done.4
  14.4 3.7 fusion
  18.0 0.0 all-reduce.7.cloned.1.call-update
  18.0 0.0 all-gather.4.cloned.1.call-start
  18.1 0.0 copy-done.8
  18.1 0.6 dynamic-slice.1
  19.4 270.8 %all-reduce.5.cloned.1.call-done = f32[256,6144]{1,0:T(8,128)} async-done(((f32[256,6144]{1,0:T(8,128)}), f32[256,6144]{1,0:T(8,128)}) %all-reduce.5.cloned.1.call-update) | async-done | bytes 6291472
  290.1 1.6 multiply_reduce_fusion.1
  291.7 794.9 %all-reduce.7.cloned.1.call-done = f32[128,6144]{1,0:T(8,128)} async-done(((f32[128,6144]{1,0:T(8,128)}), f32[128,6144]{1,0:T(8,128)}) %all-reduce.7.cloned.1.call-update) | async-done | bytes 3145744
  1086.6 1.6 multiply_reduce_fusion
  1089.5 77.7 %psum.16 = f32[]{:T(128)} all-reduce(f32[]{:T(128)S(6)} %add.44), channel_id=1, replica_groups=mesh['expert'=4,'dp'=64] {'expert','dp'}, use_global_device_ids=true, to_apply=%region_2.0 | all-reduce | flops 1 | bytes 8 | tf_op jit(solution)/shard_map/psum | solution.py:47
  1167.9 0.0 copy-done.1
  1167.9 0.0 copy-done.2
  1167.9 0.0 copy-done.3
  1168.0 1.8 fusion.6
  1169.7 0.7 copy.20
  1170.4 0.0 all-gather.4.cloned.1.call-update
  1170.4 0.0 all-gather.6.cloned.1.call-start
  1170.4 0.0 copy-done.5
  1170.5 0.0 copy-done.6
  1170.5 0.0 copy-done.7
  1170.5 1.8 convert_bitcast_fusion
  1172.2 0.0 all-gather.6.cloned.1.call-update
  1172.3 83.1 %all-gather.4.cloned.1.call-done = bf16[1,128,6144]{2,0,1:T(2,128)(2,1)} async-done(((bf16[1,2,6144]{2,0,1:T(2,128)(2,1)}), bf16[1,128,6144]{2,0,1:T(2,128)(2,1)}) %all-gather.4.cloned.1.call-update) | async-done | bytes 1572880 | tf_op jit(solution)/shard_map/all_gather | solution.py:55
  1255.4 3.9 copy.21
  1259.3 409.6 %all-gather.6.cloned.1.call-done = bf16[256,1,6144]{2,1,0:T(2,128)(2,1)} async-done(((bf16[1,1,6144]{2,1,0:T(2,128)(2,1)}), bf16[256,1,6144]{2,1,0:T(2,128)(2,1)}) %all-gather.6.cloned.1.call-update) | async-done | bytes 3145744 | tf_op jit(solution)/shard_map/all_gather | solution.py:54
  1668.9 6.2 copy.24
Async XLA Ops:
  7.2 1.9 copy-start
  7.2 283.0 %all-reduce.5.cloned.1.call-start = ((), (), s32[]{:S(2)}) async-start(), calls=%async_computation.2 | async-start | bytes 12582912
  13.6 0.8 copy-start.4
  13.6 4.5 copy-start.8
  13.6 1154.3 %copy-start.1 = (f32[1,2,6144]{2,1,0:T(2,128)S(1)}, f32[1,2,6144]{2,1,0:T(2,128)}, u32[]{:S(2)}) copy-start(f32[1,2,6144]{2,1,0:T(2,128)} %param.17) | copy-start | bytes 147460
  13.7 1154.3 %copy-start.2 = (f32[1,2,6144]{2,1,0:T(2,128)S(1)}, f32[1,2,6144]{2,1,0:T(2,128)}, u32[]{:S(2)}) copy-start(f32[1,2,6144]{2,1,0:T(2,128)} %param.18) | copy-start | bytes 147460
  13.7 1154.3 %copy-start.3 = (f32[1,2,6144]{2,1,0:T(2,128)S(1)}, f32[1,2,6144]{2,1,0:T(2,128)}, u32[]{:S(2)}) copy-start(f32[1,2,6144]{2,1,0:T(2,128)} %param.19) | copy-start | bytes 147460
  13.7 1156.8 %copy-start.5 = (f32[1,6144]{1,0:T(1,128)S(1)}, f32[1,6144]{1,0:T(1,128)}, u32[]{:S(2)}) copy-start(f32[1,6144]{1,0:T(1,128)} %param.14) | copy-start | bytes 73732
  13.7 1156.8 %copy-start.6 = (f32[1,6144]{1,0:T(1,128)S(1)}, f32[1,6144]{1,0:T(1,128)}, u32[]{:S(2)}) copy-start(f32[1,6144]{1,0:T(1,128)} %param.15) | copy-start | bytes 73732
  13.7 1156.8 %copy-start.7 = (f32[1,6144]{1,0:T(1,128)S(1)}, f32[1,6144]{1,0:T(1,128)}, u32[]{:S(2)}) copy-start(f32[1,6144]{1,0:T(1,128)} %param.16) | copy-start | bytes 73732
  13.7 1072.9 %all-reduce.7.cloned.1.call-start = ((), (), s32[]{:S(2)}) async-start(), calls=%async_computation.3 | async-start | bytes 6291456
  18.0 1237.3 %all-gather.4.cloned.1.call-start = ((), (), s32[]{:S(2)}) async-start(), calls=%async_computation | async-start | bytes 3194880 | tf_op jit(solution)/shard_map/all_gather | solution.py:55
  1170.4 498.5 %all-gather.6.cloned.1.call-start = ((), (), s32[]{:S(2)}) async-start(), calls=%async_computation.1 | async-start | bytes 6316032 | tf_op jit(solution)/shard_map/all_gather | solution.py:54
Sparse Core Ops, SparseCore 0:
  13.7 276.3 all-reduce.4
  293.5 793.0 all-reduce.6
  1170.5 84.8 all-gather.3
  1257.7 411.1 all-gather.5
where the time goes:
time: 1680 us
  waiting for transfers between devices  1560 us (93%)
  blocking collectives  77.7 us (5%)
    unnamed x6, waiting for transfers between devices  1070 us
    all_gather x1, waiting for transfers between devices, body(): attn_full = lax.all_gather(attn_half, ('expert', 'dp'), axis=0, tiled=True)  410 us
    all_gather x1, waiting for transfers between devices, body(): lax.all_gather(we_new.astype(jnp.bfloat16), 'dp', axis=1, tiled=True)  83.1 us
    psum x1, blocking collectives, body(): summed = lax.psum((sq_attn, sq_exp), ('expert', 'dp'))  77.7 us
  transfers between devices with their start and end apart: 4, of which 4 were waited for; matrix products, arithmetic and copies ran while one was open for 1% of the time, Pallas kernels for 0%

commit v1 on v0

v1 whole, which is shorter than its diff:
```python
import math

import jax
import jax.numpy as jnp
from jax import lax
from jax.experimental import pallas as pl
from jax.experimental.pallas import tpu as pltpu
from jax.sharding import PartitionSpec as P

beta_first = 0.9
beta_second = 0.95
bias_first = 1.0 - 0.9**10
bias_second = 1.0 - 0.95**10
learn_rate = 0.01
decay_rate = 0.1
adam_eps = 1e-08

MESH = pl.DeviceIdType.MESH
F32 = jnp.float32
BF16 = jnp.bfloat16
HALF = 3072
PART = 1536
LANES = 128
ROWS = HALF // LANES
PROWS = PART // LANES
STEP = 512


def adamw(grad, weight, moment, second, factor):
    scaled = factor * grad
    moment_new = beta_first * moment + (1.0 - beta_first) * scaled
    second_new = beta_second * second + (1.0 - beta_second) * scaled * scaled
    update = moment_new / bias_first / (jnp.sqrt(second_new / bias_second) + adam_eps)
    weight_new = weight - learn_rate * (update + decay_rate * weight)
    return (weight_new, moment_new, second_new)


def grouped(row):
    low = row & 3
    x = (row >> 2) & 3
    y = (row >> 4) & 3
    z_lo = row >> 6
    return ((y * 4 + x) * 4 + z_lo) * 4 + low


def device_at(z, y, x, core):
    return (lax.rem(z, 4), ((y * 4 + x) * 2 + lax.div(z, 4)) * 2 + core)


def aligned(index, multiple):
    return pl.multiple_of(index, multiple)


def comm_kernel(
    limit,
    act_a, dy_a, act_e, dy_e, w_a, m_a, v_a, w_e, m_e, v_e,
    g_out, f_out, full_a, full_e,
    lhs_a, lhs_e,
    cs_a, cs_e, cr_a, cr_e,
    own_a, own_e, s1_a, s1_e, r1_a, r1_e,
    own2_a, own2_e, s2_a, s2_e, r2_a, r2_e,
    s3_a, s3_e, r3_a, r3_e,
    n_s, n_r,
    ws_a, ws_e, g3_a, g3_e, gt_a, gt_e,
    send_sem, recv_sem, local_sem,
):
    z_lo = lax.axis_index("expert")
    dp = lax.axis_index("dp")
    core = lax.rem(dp, 2)
    z_hi = lax.rem(lax.div(dp, 2), 2)
    x = lax.rem(lax.div(dp, 4), 4)
    y = lax.div(dp, 16)
    z = z_hi * 4 + z_lo
    other = 1 - core

    def zc_mate(dz, dc):
        oz = lax.rem(z + dz, 8)
        oc = core if dc == 0 else other
        return oz, oc

    def plane_mate(dy, dx):
        return device_at(z, lax.rem(y + dy, 4), lax.rem(x + dx, 4), core)

    barrier = pltpu.get_barrier_semaphore()
    greeted = 0
    for dz in range(8):
        for dc in range(2):
            if dz or dc:
                oz, oc = zc_mate(dz, dc)
                pl.semaphore_signal(barrier, inc=1, device_id=device_at(oz, y, x, oc), device_id_type=MESH)
                greeted += 1
    for dy in range(4):
        for dx in range(4):
            if dy or dx:
                pl.semaphore_signal(barrier, inc=1, device_id=plane_mate(dy, dx), device_id_type=MESH)
                greeted += 1

    sent = []

    def send(src, dst, where):
        i = len(sent)
        copy = pltpu.make_async_remote_copy(
            src_ref=src, dst_ref=dst, send_sem=send_sem.at[i], recv_sem=recv_sem.at[i],
            device_id=where, device_id_type=MESH,
        )
        copy.start()
        sent.append(copy)
        return copy

    kept = []

    def keep(src, dst):
        copy = pltpu.make_async_copy(src, dst, local_sem.at[len(kept)])
        copy.start()
        kept.append(copy)

    r0 = lax.broadcasted_iota(jnp.int32, (256, 256), 0)
    r1 = lax.broadcasted_iota(jnp.int32, (256, 256), 1)
    pick = jnp.where(r0 == grouped(r1), 1.0, 0.0).astype(BF16)
    lhs_a[...] = lax.dot_general(
        pick, act_a[...], (((1,), (1,)), ((), ())), preferred_element_type=F32
    ).astype(BF16)
    e0 = lax.broadcasted_iota(jnp.int32, (128, 128), 0)
    e1 = lax.broadcasted_iota(jnp.int32, (128, 128), 1)
    same = jnp.where(e0 == e1, 1.0, 0.0).astype(BF16)
    lhs_e[...] = lax.dot_general(
        same, act_e[0], (((1,), (1,)), ((), ())), preferred_element_type=F32
    ).astype(BF16)

    def product(lhs, rhs):
        return jnp.dot(lhs, rhs, preferred_element_type=F32)

    copies_c = []
    for part in range(2):
        def other_terms(i, carry):
            at = aligned(i * STEP, STEP)
            col = aligned(other * HALF + part * PART + i * STEP, STEP)
            ga = product(lhs_a[...], dy_a[:, pl.ds(col, STEP)])
            cs_a[part, :, :, pl.ds(at, STEP)] = ga.astype(BF16).reshape(16, 16, STEP)
            ge = product(lhs_e[...], dy_e[0, :, pl.ds(col, STEP)])
            cs_e[part, :, :, pl.ds(at, STEP)] = ge.astype(BF16).reshape(16, 8, STEP)
            return carry

        lax.fori_loop(0, PART // STEP, other_terms, 0)
        if part == 0:
            pl.semaphore_wait(barrier, greeted)
        peer = device_at(z, y, x, other)
        copies_c.append((
            send(cs_a.at[part], cr_a.at[part], peer),
            send(cs_e.at[part], cr_e.at[part], peer),
        ))

    copies_1 = []
    for part in range(2):
        for copy in copies_c[part]:
            copy.wait_recv()

        def own_terms(i, carry):
            at = aligned(i * STEP, STEP)
            col = aligned(core * HALF + part * PART + i * STEP, STEP)
            ga = product(lhs_a[...], dy_a[:, pl.ds(col, STEP)]).reshape(16, 16, STEP)
            ga = ga + cr_a[part, :, :, pl.ds(at, STEP)].astype(F32)
            ga = ga.reshape(4, 4, 16, STEP)
            own_a[part, :, :, :, pl.ds(at, STEP)] = ga
            s1_a[part, :, :, :, pl.ds(at, STEP)] = ga.astype(BF16)
            ge = product(lhs_e[...], dy_e[0, :, pl.ds(col, STEP)]).reshape(16, 8, STEP)
            ge = ge + cr_e[part, :, :, pl.ds(at, STEP)].astype(F32)
            ge = ge.reshape(4, 4, 8, STEP)
            own_e[part, :, :, :, pl.ds(at, STEP)] = ge
            s1_e[part, :, :, :, pl.ds(at, STEP)] = ge.astype(BF16)
            return carry

        lax.fori_loop(0, PART // STEP, own_terms, 0)
        batch = []
        for d in (2, 1, 3):
            for s1, r1 in ((s1_a, r1_a), (s1_e, r1_e)):
                if part == 0:
                    ox = lax.rem(x + d, 4)
                    batch.append(send(s1.at[0, :, ox], r1.at[0, d - 1], plane_mate(0, d)))
                else:
                    oy = lax.rem(y + d, 4)
                    batch.append(send(s1.at[1, oy], r1.at[1, d - 1], plane_mate(d, 0)))
        copies_1.append(batch)

    copies_2 = []
    for part in range(2):
        for copy in copies_1[part]:
            copy.wait_recv()

        def sum_first(b, carry):
            for own, r1, own2, s2 in ((own_a, r1_a, own2_a, s2_a), (own_e, r1_e, own2_e, s2_e)):
                total = own[0, b, x] if part == 0 else own[1, y, b]
                for d in range(3):
                    total = total + r1[part, d, b].astype(F32)
                own2[part, b] = total
                s2[part, b] = total.astype(BF16)
            return carry

        lax.fori_loop(0, 4, sum_first, 0)
        batch = []
        for d in (2, 1, 3):
            for s2, r2 in ((s2_a, r2_a), (s2_e, r2_e)):
                if part == 0:
                    oy = lax.rem(y + d, 4)
                    batch.append(send(s2.at[0, oy], r2.at[0, d - 1], plane_mate(d, 0)))
                else:
                    ox = lax.rem(x + d, 4)
                    batch.append(send(s2.at[1, ox], r2.at[1, d - 1], plane_mate(0, d)))
        copies_2.append(batch)

    for part in range(2):
        for copy in copies_2[part]:
            copy.wait_recv()
        mine = y if part == 0 else x
        for own2, r2, s3, rows in ((own2_a, r2_a, s3_a, 16), (own2_e, r2_e, s3_e, 8)):
            total = own2[part, mine]
            for d in range(3):
                total = total + r2[part, d].astype(F32)
            for t in range(PROWS):
                s3[pl.ds(part * PROWS + t, rows, stride=ROWS), :] = total[:, t * LANES : (t + 1) * LANES]

    copies_3 = []
    for dz in (4, 3, 5, 2, 6, 1, 7, 0):
        for dc in range(2):
            if dz or dc:
                oz, oc = zc_mate(dz, dc)
                q = lax.rem(oz, 4) * 4 + lax.div(oz, 4) * 2 + oc
                copies_3.append(send(
                    s3_a.at[pl.ds(aligned(q * ROWS, 8), ROWS)], r3_a.at[dc, dz], device_at(oz, y, x, oc)
                ))
            if dz in (0, 4) and (dz or dc):
                q = lax.div(oz, 4) * 2 + oc
                copies_3.append(send(
                    s3_e.at[pl.ds(aligned(q * 2 * ROWS, 8), 2 * ROWS)],
                    r3_e.at[dc, dz // 4],
                    device_at(oz, y, x, oc),
                ))
    for copy in copies_3:
        copy.wait_recv()

    my_q = z_lo * 4 + z_hi * 2 + core
    my_e = z_hi * 2 + core
    near = s3_a[pl.ds(aligned(my_q * ROWS, 8), ROWS), :]
    far = r3_a[1, 0]
    for dz in range(1, 8):
        near = near + r3_a[0, dz]
        far = far + r3_a[1, dz]
    near_at = pl.ds(aligned(core * ROWS, 8), ROWS)
    far_at = pl.ds(aligned(other * ROWS, 8), ROWS)
    g_out[0, near_at, :] = near
    g_out[0, far_at, :] = far
    near_e = s3_e[pl.ds(aligned(my_e * 2 * ROWS, 8), 2 * ROWS), :] + r3_e[0, 1]
    far_e = r3_e[1, 0] + r3_e[1, 1]
    for j in range(2):
        g_out[1 + j, near_at, :] = near_e[j * ROWS : (j + 1) * ROWS]
        g_out[1 + j, far_at, :] = far_e[j * ROWS : (j + 1) * ROWS]

    square = jnp.zeros((8, LANES), F32)
    for piece in (near, far, near_e, far_e):
        for i in range(piece.shape[0] // 8):
            block = piece[i * 8 : (i + 1) * 8]
            square = square + block * block
    n_s[0] = square
    batch = []
    for dz in (4, 3, 5, 2, 6, 1, 7, 0):
        for dc in range(2):
            if dz or dc:
                oz, oc = zc_mate(dz, dc)
                batch.append(send(n_s.at[0], n_r.at[0, dz * 2 + dc], device_at(oz, y, x, oc)))
    for copy in batch:
        copy.wait_recv()
    for i in range(1, 16):
        square = square + n_r[0, i]
    n_s[1] = square
    batch = []
    for dy in (2, 1, 3, 0):
        for dx in (2, 1, 3, 0):
            if dy or dx:
                batch.append(send(n_s.at[1], n_r.at[1, dy * 4 + dx], plane_mate(dy, dx)))
    for copy in batch:
        copy.wait_recv()
    for i in range(1, 16):
        square = square + n_r[1, i]
    norm = jnp.sqrt(jnp.sum(square, keepdims=True))
    factor = jnp.minimum(1.0, limit / (norm + 1e-06))
    f_out[...] = jnp.broadcast_to(factor, (8, LANES))

    weight_a = adamw(g_out[0], w_a[...], m_a[...], v_a[...], factor)[0]
    for h in range(2):
        ws_a[h] = weight_a[h * ROWS : (h + 1) * ROWS]
    for j in range(2):
        rows = pl.ds(j, 2 * ROWS, stride=2)
        weight_e = adamw(g_out[1 + j], w_e[rows, :], m_e[rows, :], v_e[rows, :], factor)[0]
        for h in range(2):
            ws_e[h, pl.ds(j * ROWS, ROWS), :] = weight_e[h * ROWS : (h + 1) * ROWS]

    at_a = pl.ds(aligned(my_q * ROWS, 8), ROWS)
    at_e = pl.ds(aligned(my_e * 2 * ROWS, 8), 2 * ROWS)
    batch = []
    for dz in (4, 3, 5, 2, 6, 1, 7, 0):
        for dc in range(2):
            if dz or dc:
                oz, oc = zc_mate(dz, dc)
                batch.append(send(ws_a.at[oc], g3_a.at[at_a], device_at(oz, y, x, oc)))
            if dz in (0, 4) and (dz or dc):
                batch.append(send(ws_e.at[oc], g3_e.at[at_e], device_at(oz, y, x, oc)))
    g3_a[at_a, :] = ws_a[core]
    g3_e[at_e, :] = ws_e[core]
    for copy in batch:
        copy.wait_recv()
    for part in range(2):
        for t in range(PROWS):
            lanes = pl.ds(t * LANES, LANES)
            gt_a[part, y, x, :, lanes] = g3_a[pl.ds(part * PROWS + t, 16, stride=ROWS), :].astype(BF16)
            gt_e[part, y, x, :, lanes] = g3_e[pl.ds(part * PROWS + t, 8, stride=ROWS), :].astype(BF16)

    copies_2 = []
    for part in range(2):
        batch = []
        for d in (2, 1, 3):
            for gt in (gt_a, gt_e):
                where = plane_mate(d, 0) if part == 0 else plane_mate(0, d)
                batch.append(send(gt.at[part, y, x], gt.at[part, y, x], where))
        copies_2.append(batch)
    copies_1 = []
    peer = device_at(z, y, x, other)
    landed = []

    def deliver(part, index):
        for gt, full in ((gt_a, full_a), (gt_e, full_e)):
            if part == 0:
                src, dst = gt.at[0, :, index], full.at[core, 0, :, index]
            else:
                src, dst = gt.at[1, index], full.at[core, 1, index]
            landed.append(send(src, dst, peer))
            keep(src, dst)

    for part in range(2):
        for copy in copies_2[part]:
            copy.wait_recv()
        batch = {}
        for d in (2, 1, 3):
            for gt in (gt_a, gt_e):
                if part == 0:
                    copy = send(gt.at[0, :, x], gt.at[0, :, x], plane_mate(0, d))
                else:
                    copy = send(gt.at[1, y], gt.at[1, y], plane_mate(d, 0))
                batch.setdefault(d, []).append(copy)
        copies_1.append(batch)
        deliver(part, x if part == 0 else y)
    for d in (1, 3, 2):
        for part in range(2):
            for copy in copies_1[part][d]:
                copy.wait_recv()
            deliver(part, lax.rem((x if part == 0 else y) + 4 - d, 4))

    for copy in landed:
        copy.wait_recv()
    for copy in kept:
        copy.wait()
    for copy in sent:
        copy.wait_send()


def finish_kernel(
    full_a, full_e, g, f, w_a, m_a, v_a, w_e, m_e, v_e,
    wa_o, ma_o, va_o, we_o, me_o, ve_o, attn_o, exp_o, pick,
):
    @pl.when(pl.program_id(0) == 0)
    def _():
        r0 = lax.broadcasted_iota(jnp.int32, (256, 256), 0)
        r1 = lax.broadcasted_iota(jnp.int32, (256, 256), 1)
        pick[...] = jnp.where(grouped(r0) == r1, 1.0, 0.0).astype(BF16)
        factor = f[0:1, 0:1]
        new = adamw(g[0], w_a[...], m_a[...], v_a[...], factor)
        for ref, value in zip((wa_o, ma_o, va_o), new):
            ref[...] = value
        for j in range(2):
            rows = pl.ds(j, 2 * ROWS, stride=2)
            new = adamw(g[1 + j], w_e[rows, :], m_e[rows, :], v_e[rows, :], factor)
            for ref, value in zip((we_o, me_o, ve_o), new):
                ref[rows, :] = value

    attn_o[...] = jnp.dot(pick[...], full_a[0], preferred_element_type=F32).astype(BF16)
    exp_o[0] = full_e[0]


def body(act_attn, dy_attn, act_exp, dy_exp, w_attn, m_attn, v_attn, w_exp, m_exp, v_exp):
    width = w_attn.shape[1]
    total_params = width * (act_attn.shape[1] + lax.axis_size("expert") * act_exp.shape[2])
    limit = 0.5 * math.sqrt(total_params)
    attn_state = [v.reshape(2 * ROWS, LANES) for v in (w_attn, m_attn, v_attn)]
    exp_state = [
        v.reshape(2, 2 * ROWS, LANES).transpose(1, 0, 2).reshape(4 * ROWS, LANES)
        for v in (w_exp, m_exp, v_exp)
    ]
    vmem = pl.BlockSpec(memory_space=pltpu.VMEM)
    anywhere = pl.BlockSpec(memory_space=pl.ANY)

    def pair(shape, dtype, *lead):
        return [pltpu.VMEM(lead + (16,) + shape, dtype), pltpu.VMEM(lead + (8,) + shape, dtype)]

    n_send = 160
    g, f, full_a, full_e = pl.pallas_call(
        lambda *refs: comm_kernel(limit, *refs),
        out_shape=(
            jax.ShapeDtypeStruct((3, 2 * ROWS, LANES), F32),
            jax.ShapeDtypeStruct((8, LANES), F32),
            jax.ShapeDtypeStruct((2, 2, 4, 4, 16, PART), BF16),
            jax.ShapeDtypeStruct((2, 2, 4, 4, 8, PART), BF16),
        ),
        in_specs=[vmem] * 10,
        out_specs=(vmem, vmem, anywhere, anywhere),
        scratch_shapes=[
            pltpu.VMEM((256, 256), BF16),
            pltpu.VMEM((128, 128), BF16),
            *pair((PART,), BF16, 2, 16),
            *pair((PART,), BF16, 2, 16),
            *pair((PART,), F32, 2, 4, 4),
            *pair((PART,), BF16, 2, 4, 4),
            *pair((PART,), BF16, 2, 3, 4),
            *pair((PART,), F32, 2, 4),
            *pair((PART,), BF16, 2, 4),
            *pair((PART,), BF16, 2, 3),
            pltpu.VMEM((16 * ROWS, LANES), F32),
            pltpu.VMEM((8 * ROWS, LANES), F32),
            pltpu.VMEM((2, 8, ROWS, LANES), F32),
            pltpu.VMEM((2, 2, 2 * ROWS, LANES), F32),
            pltpu.VMEM((2, 8, LANES), F32),
            pltpu.VMEM((2, 16, 8, LANES), F32),
            pltpu.VMEM((2, ROWS, LANES), F32),
            pltpu.VMEM((2, 2 * ROWS, LANES), F32),
            pltpu.VMEM((16 * ROWS, LANES), F32),
            pltpu.VMEM((8 * ROWS, LANES), F32),
            *pair((PART,), BF16, 2, 4, 4),
            pltpu.SemaphoreType.DMA((n_send,)),
            pltpu.SemaphoreType.DMA((n_send,)),
            pltpu.SemaphoreType.DMA((16,)),
        ],
        compiler_params=pltpu.CompilerParams(
            collective_id=0, has_side_effects=True, vmem_limit_bytes=48 * 1024 * 1024
        ),
    )(act_attn, dy_attn, act_exp, dy_exp, *attn_state, *exp_state)

    steps = width // STEP
    per_part = PART // STEP
    whole = lambda shape: pl.BlockSpec(shape, lambda i: (0,) * len(shape))
    a_shape, e_shape = (2 * ROWS, LANES), (4 * ROWS, LANES)
    outs = pl.pallas_call(
        finish_kernel,
        grid=(steps,),
        out_shape=(
            *[jax.ShapeDtypeStruct(a_shape, F32)] * 3,
            *[jax.ShapeDtypeStruct(e_shape, F32)] * 3,
            jax.ShapeDtypeStruct((256, width), BF16),
            jax.ShapeDtypeStruct((1, 128, width), BF16),
        ),
        in_specs=[
            pl.BlockSpec((1, 256, STEP), lambda i: (i // per_part, 0, i % per_part)),
            pl.BlockSpec((1, 128, STEP), lambda i: (i // per_part, 0, i % per_part)),
            whole((3, 2 * ROWS, LANES)),
            whole((8, LANES)),
            *[whole(a_shape)] * 3,
            *[whole(e_shape)] * 3,
        ],
        out_specs=(
            *[whole(a_shape)] * 3,
            *[whole(e_shape)] * 3,
            pl.BlockSpec((256, STEP), lambda i: (0, i)),
            pl.BlockSpec((1, 128, STEP), lambda i: (0, 0, i)),
        ),
        scratch_shapes=[pltpu.VMEM((256, 256), BF16)],
    )(full_a.reshape(4, 256, PART), full_e.reshape(4, 128, PART), g, f, *attn_state, *exp_state)
    attn_new = [v.reshape(1, width) for v in outs[:3]]
    exp_new = [
        v.reshape(2 * ROWS, 2, LANES).transpose(1, 0, 2).reshape(1, 2, width) for v in outs[3:6]
    ]
    return (*attn_new, *exp_new, outs[6], outs[7])


def solution(mesh):
    rows = P(("expert", "dp"), None)
    owned = P("expert", "dp", None)
    return jax.shard_map(
        body,
        mesh=mesh,
        in_specs=(rows, rows, owned, owned, rows, rows, rows, owned, owned, owned),
        out_specs=(rows, rows, rows, owned, owned, owned, P(), P("expert", None, None)),
        check_vma=False,
    )
```

time: 1680 us -> 113 us (0.07)
  waiting for transfers between devices: 1560 us -> 0 us
  Pallas kernels: 0 us -> 101 us
  blocking collectives: 77.7 us -> 0 us
    unnamed x6 -> x0, waiting for transfers between devices: 1070 us -> none
    all_gather x2 -> x0, waiting for transfers between devices: 493 us -> none  [the longest x1 410 us: body(): attn_full = lax.all_gather(attn_half, ('expert', 'dp'), axis=0, tiled=True)]
    pallas_call x0 -> x2, Pallas kernels: none -> 101 us  [the longest x1 91.7 us: body(): pl.pallas_call(lambda *refs: comm_kernel(limit, *refs), out_shape=(jax.Sh...]
    psum x1 -> x0, blocking collectives: 77.7 us -> none  [body(): summed = lax.psum((sq_attn, sq_exp), ('expert', 'dp'))]
  transfers between devices with their start and end apart: 4 -> 0, of which waited for: 4 -> 0; matrix products, arithmetic and copies ran while one was open for 1% -> 0% of each run, Pallas kernels for 0% -> 0%
where the time goes in v1:
time: 113 us; the launch traced here: 112 us
  Pallas kernels  101 us (89%)
  local copies, waits for them, and re-layouts  10 us (9%)
    pallas_call x1, Pallas kernels, body(): pl.pallas_call(lambda *refs: comm_kernel(limit, *refs), out_shape=(jax.Sh...  91.7 us
    unnamed x24, local copies, waits for them, and re-layouts  10 us
    pallas_call x1, Pallas kernels, body(): pl.pallas_call(finish_kernel, grid=(steps,), out_shape=(*[jax.ShapeDtypeS...  9.6 us

profile of v1, /device:TPU:1, one launch (start us, length us, event | category | flops | bytes accessed | tf_op | source)
XLA Modules:
  0.0 112.0 jit_solution(16396513946525760950)
XLA Ops:
  0.6 0.0 copy-start
  0.6 1.4 %copy-done = bf16[1,128,6144]{2,1,0:T(8,128)(2,1)S(1)} copy-done((bf16[1,128,6144]{2,1,0:T(8,128)(2,1)S(1)}, bf16[1,128,6144]{2,1,0:T(8,128)(2,1)}, u32[]{:S(2)}) %copy-start) | copy-done | bytes 1572888
  2.0 0.0 copy-start.2
  2.0 0.8 copy-done.2
  2.8 0.0 copy-start.3
  2.8 0.8 copy-done.3
  3.6 0.0 copy-start.4
  3.6 0.8 copy-done.4
  4.4 0.0 copy-start.5
  4.4 0.9 copy-done.5
  5.3 0.0 copy-start.6
  5.3 0.7 copy-done.6
  6.1 0.0 copy-start.7
  6.1 0.7 copy-done.7
  6.8 0.0 copy-start.8
  6.8 0.7 copy-done.8
  7.6 0.0 copy-start.10
  7.6 0.8 copy-done.10
  8.3 91.7 %shard_map.161 = (f32[3,48,128]{2,1,0:T(8,128)S(1)}, f32[8,128]{1,0:T(8,128)S(1)}, bf16[2,2,4,4,16,1536]{5,4,3,2,1,0:T(8,128)(2,1)}, bf16[2,2,4,4,8,1536]{5,4,3,2,1,0:T(8,128)(2,1)S(1)}) custom-call(bf16[256,256]{1,0:T(8,128)(2,1)S(1)} %copy-done.5, bf16[256,6144]{1,0:T(8,128)(2,1)} %refs_1_.1, bf16[1,128,128]{2,1,0:T(8,128)(2,1)S(1)} %copy-done.10, ...), custom_call_target="tpu_custom_call" | custom-call | tf_op jit(solution)/shard_map/pallas_call | solution.py:404
  100.0 0.0 copy-start.1
  100.0 1.2 %copy-done.1 = bf16[2,2,4,4,8,1536]{5,4,3,2,1,0:T(8,128)(2,1)} copy-done((bf16[2,2,4,4,8,1536]{5,4,3,2,1,0:T(8,128)(2,1)}, bf16[2,2,4,4,8,1536]{5,4,3,2,1,0:T(8,128)(2,1)S(1)}, u32[]{:S(2)}) %copy-start.1) | copy-done | bytes 1572888
  101.2 0.0 copy-start.9
  101.2 0.6 copy-done.9
  101.8 0.0 copy-start.11
  101.8 0.6 copy-done.11
  102.4 9.6 %shard_map.162 = (f32[48,128]{1,0:T(8,128)}, f32[48,128]{1,0:T(8,128)}, f32[48,128]{1,0:T(8,128)}, f32[96,128]{1,0:T(8,128)}, f32[96,128]{1,0:T(8,128)}, /*index...) custom-call(bf16[4,256,1536]{2,1,0:T(8,128)(2,1)} %bitcast.51, ...), custom_call_target="tpu_custom_call" | custom-call | tf_op jit(solution)/shard_map/pallas_call | solution.py:449
Async XLA Ops:
  0.6 1.4 %copy-start = (bf16[1,128,6144]{2,1,0:T(8,128)(2,1)S(1)}, bf16[1,128,6144]{2,1,0:T(8,128)(2,1)}, u32[]{:S(2)}) copy-start(bf16[1,128,6144]{2,1,0:T(8,128)(2,1)} %refs_3_.1) | copy-start | bytes 4718596
  2.0 0.8 copy-start.2
  2.8 0.8 copy-start.3
  3.6 0.8 copy-start.4
  4.4 0.9 copy-start.5
  5.3 0.7 copy-start.6
  6.1 0.7 copy-start.7
  6.8 0.7 copy-start.8
  7.6 0.8 copy-start.10
  100.0 1.2 %copy-start.1 = (bf16[2,2,4,4,8,1536]{5,4,3,2,1,0:T(8,128)(2,1)}, bf16[2,2,4,4,8,1536]{5,4,3,2,1,0:T(8,128)(2,1)S(1)}, u32[]{:S(2)}) copy-start(bf16[2,2,4,4,8,1536]{5,4,3,2,1,0:T(8,128)(2,1)S(1)} %get-tuple-element.21) | copy-start | bytes 4718596
  101.2 0.6 copy-start.9
  101.8 0.6 copy-start.11

commit v2 on v1

v2 whole, which is shorter than its diff:
```python
import math

import jax
import jax.numpy as jnp
from jax import lax
from jax.experimental import pallas as pl
from jax.experimental.pallas import tpu as pltpu
from jax.sharding import PartitionSpec as P

beta_first = 0.9
beta_second = 0.95
bias_first = 1.0 - 0.9**10
bias_second = 1.0 - 0.95**10
learn_rate = 0.01
decay_rate = 0.1
adam_eps = 1e-08

MESH = pl.DeviceIdType.MESH
F32 = jnp.float32
BF16 = jnp.bfloat16
HALF = 3072
PART = 1536
LANES = 128
ROWS = HALF // LANES
PROWS = PART // LANES
STEP = 512
WIDE = 768

def adamw(grad, weight, moment, second, factor):
    scaled = factor * grad
    moment_new = beta_first * moment + (1.0 - beta_first) * scaled
    second_new = beta_second * second + (1.0 - beta_second) * scaled * scaled
    update = moment_new / bias_first / (jnp.sqrt(second_new / bias_second) + adam_eps)
    weight_new = weight - learn_rate * (update + decay_rate * weight)
    return (weight_new, moment_new, second_new)

def grouped(row):
    low = row & 3
    x = (row >> 2) & 3
    y = (row >> 4) & 3
    z_lo = row >> 6
    return ((y * 4 + x) * 4 + z_lo) * 4 + low

def device_at(z, y, x, core):
    return (lax.rem(z, 4), ((y * 4 + x) * 2 + lax.div(z, 4)) * 2 + core)

def aligned(index, multiple):
    return pl.multiple_of(index, multiple)

def comm_kernel(
    limit,
    act_a_hbm, dy_a_hbm, act_e_hbm, dy_e_hbm, w_a_hbm, m_a_hbm, v_a_hbm, w_e_hbm, m_e_hbm, v_e_hbm,
    g_hbm, f_hbm, full,
    act_a, dy_a, act_e, dy_e, w_a, m_a, v_a, w_e, m_e, v_e, g_out, f_out,
    lhs_a, lhs_e,
    cs, cr, own, s1, r1, own2, s2, r2,
    s3_a, s3_e, z3_a, z3_e, r3_a, r3_e,
    n_s, n_r,
    ws_a, ws_e, gr_a, gr_e, g3_a, g3_e, gt,
    send_sem, recv_sem, local_sem,
):
    z_lo = lax.axis_index("expert")
    dp = lax.axis_index("dp")
    core = lax.rem(dp, 2)
    z_hi = lax.rem(lax.div(dp, 2), 2)
    x = lax.rem(lax.div(dp, 4), 4)
    y = lax.div(dp, 16)
    z = z_hi * 4 + z_lo
    other = 1 - core
    peer = device_at(z, y, x, other)

    def zc_mate(dz, dc):
        oz = lax.rem(z + dz, 8)
        oc = core if dc == 0 else other
        return oz, oc

    def plane_mate(dy, dx):
        return device_at(z, lax.rem(y + dy, 4), lax.rem(x + dx, 4), core)

    def axis_mate(axis, d):
        return plane_mate(d, 0) if axis == 0 else plane_mate(0, d)

    place = (y, x)

    kept = []
    waited = []

    def keep(src, dst):
        copy = pltpu.make_async_copy(src, dst, local_sem.at[len(kept)])
        copy.start()
        kept.append(copy)
        return copy

    def need(copies):
        for copy in copies:
            copy.wait()
            waited.append(copy)

    sent = []
    arrived = []

    def send(src, dst, where):
        i = len(sent)
        copy = pltpu.make_async_remote_copy(
            src_ref=src, dst_ref=dst, send_sem=send_sem.at[i], recv_sem=recv_sem.at[i],
            device_id=where, device_id_type=MESH,
        )
        copy.start()
        sent.append(copy)
        return copy

    def arrive(copies):
        for copy in copies:
            copy.wait_recv()
            arrived.append(copy)

    def finish_all():
        arrive([copy for copy in sent if not any(copy is done for done in arrived)])
        for copy in kept[len(waited):]:
            copy.wait()
        for copy in sent:
            copy.wait_send()

    need_act = (keep(act_a_hbm, act_a), keep(act_e_hbm.at[0], act_e))
    need_dy = []
    for half in (other, core):
        for part in range(2):
            cols = pl.ds(aligned(half * HALF + part * PART, PART), PART)
            need_dy.append((
                keep(dy_a_hbm.at[:, cols], dy_a.at[:, cols]),
                keep(dy_e_hbm.at[0, :, cols], dy_e.at[:, cols]),
            ))
    need_state = [
        keep(src, dst)
        for src, dst in (
            (w_a_hbm, w_a), (m_a_hbm, m_a), (v_a_hbm, v_a), (w_e_hbm, w_e), (m_e_hbm, m_e), (v_e_hbm, v_e)
        )
    ]

    barrier = pltpu.get_barrier_semaphore()
    greeted = 0
    for dz in range(8):
        for dc in range(2):
            if dz or dc:
                oz, oc = zc_mate(dz, dc)
                pl.semaphore_signal(barrier, inc=1, device_id=device_at(oz, y, x, oc), device_id_type=MESH)
                greeted += 1
    for dy in range(4):
        for dx in range(4):
            if dy or dx:
                pl.semaphore_signal(barrier, inc=1, device_id=plane_mate(dy, dx), device_id_type=MESH)
                greeted += 1

    need(need_act)
    r0 = lax.broadcasted_iota(jnp.int32, (256, 256), 0)
    r1_ = lax.broadcasted_iota(jnp.int32, (256, 256), 1)
    pick = jnp.where(r0 == grouped(r1_), 1.0, 0.0).astype(BF16)
    lhs_a[...] = lax.dot_general(
        pick, act_a[...], (((1,), (1,)), ((), ())), preferred_element_type=F32
    ).astype(BF16)
    e0 = lax.broadcasted_iota(jnp.int32, (128, 128), 0)
    e1 = lax.broadcasted_iota(jnp.int32, (128, 128), 1)
    same = jnp.where(e0 == e1, 1.0, 0.0).astype(BF16)
    lhs_e[...] = lax.dot_general(
        same, act_e[...], (((1,), (1,)), ((), ())), preferred_element_type=F32
    ).astype(BF16)

    def terms(col):
        ga = jnp.dot(lhs_a[...], dy_a[:, pl.ds(col, STEP)], preferred_element_type=F32)
        ge = jnp.dot(lhs_e[...], dy_e[:, pl.ds(col, STEP)], preferred_element_type=F32)
        return ga.reshape(4, 4, 2, 8, STEP), ge.reshape(4, 4, 8, STEP)

    copies_c = []
    for part in range(2):
        def other_terms(i, carry):
            at = pl.ds(aligned(i * STEP, STEP), STEP)
            ga, ge = terms(aligned(other * HALF + part * PART + i * STEP, STEP))
            cs[part, :, :, 0:2, :, at] = ga.astype(BF16)
            cs[part, :, :, 2, :, at] = ge.astype(BF16)
            return carry

        need(need_dy[part])
        lax.fori_loop(0, PART // STEP, other_terms, 0)
        if part == 0:
            pl.semaphore_wait(barrier, greeted)
        copies_c.append(send(cs.at[part], cr.at[part], peer))

    def block(ref, part, second, first):
        return ref.at[part, second, first] if part == 0 else ref.at[part, first, second]

    order = (2, 1, 3, 0)
    copies_1 = []
    for part in range(2):
        arrive([copies_c[part]])
        need(need_dy[2 + part])

        def own_terms(i, carry):
            at = pl.ds(aligned(i * STEP, STEP), STEP)
            ga, ge = terms(aligned(core * HALF + part * PART + i * STEP, STEP))
            ga = ga + cr[part, :, :, 0:2, :, at].astype(F32)
            own[part, :, :, 0:2, :, at] = ga
            s1[part, :, :, 0:2, :, at] = ga.astype(BF16)
            ge = ge + cr[part, :, :, 2, :, at].astype(F32)
            own[part, :, :, 2, :, at] = ge
            s1[part, :, :, 2, :, at] = ge.astype(BF16)
            return carry

        lax.fori_loop(0, PART // STEP, own_terms, 0)
        first = 1 - part
        batches = {}
        for d in order:
            at = lax.rem(place[part] + d, 4)
            batches[d] = [
                send(
                    block(s1, part, at, lax.rem(place[first] + e, 4)),
                    r1.at[part, e - 1, at],
                    axis_mate(first, e),
                )
                for e in (2, 1, 3)
            ]
        copies_1.append(batches)

    copies_2 = [[], []]
    for d in order:
        for part in range(2):
            first = 1 - part
            at = lax.rem(place[part] + d, 4)
            arrive(copies_1[part][d])
            total = block(own, part, at, place[first])[...]
            for e in range(3):
                total = total + r1[part, e, at].astype(F32)
            if d:
                s2[part, d - 1] = total.astype(BF16)
                copies_2[part].append(send(s2.at[part, d - 1], r2.at[part, d - 1], axis_mate(part, d)))
            else:
                own2[part] = total

    for part in range(2):
        arrive(copies_2[part])
        total = own2[part]
        for d in range(3):
            total = total + r2[part, d].astype(F32)
        total_a = total[0:2].reshape(16, PART)
        total_e = total[2]
        for t in range(PROWS):
            lanes = slice(t * LANES, (t + 1) * LANES)
            s3_a[pl.ds(part * PROWS + t, 16, stride=ROWS), :] = total_a[:, lanes]
            s3_e[pl.ds(part * PROWS + t, 8, stride=ROWS), :] = total_e[:, lanes]
    z3_a[...] = s3_a[...].astype(BF16).reshape(16, ROWS, LANES)
    z3_e[...] = s3_e[...].astype(BF16).reshape(4, 2 * ROWS, LANES)

    z_order = (4, 3, 5, 2, 6, 1, 7, 0)
    batch = []
    for dz in z_order:
        for dc in range(2):
            if dz or dc:
                oz, oc = zc_mate(dz, dc)
                q = lax.rem(oz, 4) * 4 + lax.div(oz, 4) * 2 + oc
                batch.append(send(z3_a.at[q], r3_a.at[dc, dz], device_at(oz, y, x, oc)))
                if dz in (0, 4):
                    q = lax.div(oz, 4) * 2 + oc
                    batch.append(send(z3_e.at[q], r3_e.at[dc, dz // 4], device_at(oz, y, x, oc)))
    arrive(batch)

    my_q = z_lo * 4 + z_hi * 2 + core
    my_e = z_hi * 2 + core
    near = s3_a[pl.ds(aligned(my_q * ROWS, 8), ROWS), :]
    far = r3_a[1, 0].astype(F32)
    for dz in range(1, 8):
        near = near + r3_a[0, dz].astype(F32)
        far = far + r3_a[1, dz].astype(F32)
    near_at = pl.ds(aligned(core * ROWS, 8), ROWS)
    far_at = pl.ds(aligned(other * ROWS, 8), ROWS)
    g_out[0, near_at, :] = near
    g_out[0, far_at, :] = far
    near_e = s3_e[pl.ds(aligned(my_e * 2 * ROWS, 8), 2 * ROWS), :] + r3_e[0, 1].astype(F32)
    far_e = r3_e[1, 0].astype(F32) + r3_e[1, 1].astype(F32)
    for j in range(2):
        g_out[1 + j, near_at, :] = near_e[j * ROWS : (j + 1) * ROWS]
        g_out[1 + j, far_at, :] = far_e[j * ROWS : (j + 1) * ROWS]

    square = jnp.zeros((8, LANES), F32)
    for piece in (near, far, near_e, far_e):
        for i in range(piece.shape[0] // 8):
            part_of = piece[i * 8 : (i + 1) * 8]
            square = square + part_of * part_of
    n_s[0] = square
    batch = []
    for dz in z_order:
        for dc in range(2):
            if dz or dc:
                oz, oc = zc_mate(dz, dc)
                batch.append(send(n_s.at[0], n_r.at[0, dz * 2 + dc], device_at(oz, y, x, oc)))
    arrive(batch)
    for i in range(1, 16):
        square = square + n_r[0, i]
    n_s[1] = square
    batch = []
    for dy in order:
        for dx in order:
            if dy or dx:
                batch.append(send(n_s.at[1], n_r.at[1, dy * 4 + dx], plane_mate(dy, dx)))
    arrive(batch)
    for i in range(1, 16):
        square = square + n_r[1, i]
    norm = jnp.sqrt(jnp.sum(square, keepdims=True))
    factor = jnp.minimum(1.0, limit / (norm + 1e-06))
    f_out[...] = jnp.broadcast_to(factor, (8, LANES))

    need(need_state)
    keep(g_out, g_hbm)
    keep(f_out, f_hbm)
    weight_a = adamw(g_out[0], w_a[...], m_a[...], v_a[...], factor)[0].astype(BF16)
    for h in range(2):
        ws_a[h] = weight_a[h * ROWS : (h + 1) * ROWS]
    for j in range(2):
        rows = pl.ds(j, 2 * ROWS, stride=2)
        weight_e = adamw(g_out[1 + j], w_e[rows, :], m_e[rows, :], v_e[rows, :], factor)[0].astype(BF16)
        for h in range(2):
            ws_e[h, pl.ds(j * ROWS, ROWS), :] = weight_e[h * ROWS : (h + 1) * ROWS]

    batch = []
    for dz in z_order:
        for dc in range(2):
            if dz or dc:
                oz, oc = zc_mate(dz, dc)
                batch.append(send(ws_a.at[oc], gr_a.at[my_q], device_at(oz, y, x, oc)))
                if dz in (0, 4):
                    batch.append(send(ws_e.at[oc], gr_e.at[my_e], device_at(oz, y, x, oc)))
    gr_a[my_q] = ws_a[core]
    gr_e[my_e] = ws_e[core]
    arrive(batch)
    g3_a[...] = gr_a[...].astype(F32).reshape(16 * ROWS, LANES)
    g3_e[...] = gr_e[...].astype(F32).reshape(8 * ROWS, LANES)
    for part in range(2):
        for t in range(PROWS):
            lanes = pl.ds(t * LANES, LANES)
            tile_a = g3_a[pl.ds(part * PROWS + t, 16, stride=ROWS), :].astype(BF16)
            gt[part, y, x, 0:2, :, lanes] = tile_a.reshape(2, 8, LANES)
            gt[part, y, x, 2, :, lanes] = g3_e[pl.ds(part * PROWS + t, 8, stride=ROWS), :].astype(BF16)

    def spread(part, at):
        here = block(gt, part, at, place[1 - part])
        return {e: send(here, here, axis_mate(1 - part, e)) for e in (2, 1, 3)}

    def deliver(part, at, first_at):
        src = block(gt, part, at, first_at)
        dst = block(full.at[core], part, at, first_at)
        send(src, dst, peer)
        keep(src, dst)

    copies_2 = [{}, {}]
    for part in range(2):
        here = gt.at[part, y, x]
        copies_2[part] = {d: send(here, here, axis_mate(part, d)) for d in (2, 1, 3)}
    copies_1 = [{0: spread(part, place[part])} for part in range(2)]
    for part in range(2):
        deliver(part, place[part], place[1 - part])
    for d in (1, 3, 2):
        for part in range(2):
            at = lax.rem(place[part] + 4 - d, 4)
            arrive([copies_2[part][d]])
            copies_1[part][d] = spread(part, at)
            deliver(part, at, place[1 - part])
    for d in (0, 1, 3, 2):
        for part in range(2):
            at = lax.rem(place[part] + 4 - d, 4)
            for e in (1, 3, 2):
                arrive([copies_1[part][d][e]])
                deliver(part, at, lax.rem(place[1 - part] + 4 - e, 4))
    finish_all()

def finish_kernel(
    full, g, f, w_a, m_a, v_a, w_e, m_e, v_e,
    wa_o, ma_o, va_o, we_o, me_o, ve_o, attn_o, exp_o, pick,
):
    @pl.when(pl.program_id(0) == 0)
    def _():
        r0 = lax.broadcasted_iota(jnp.int32, (256, 256), 0)
        r1 = lax.broadcasted_iota(jnp.int32, (256, 256), 1)
        pick[...] = jnp.where(grouped(r0) == r1, 1.0, 0.0).astype(BF16)
        factor = f[0:1, 0:1]
        new = adamw(g[0], w_a[...], m_a[...], v_a[...], factor)
        for ref, value in zip((wa_o, ma_o, va_o), new):
            ref[...] = value
        for j in range(2):
            rows = pl.ds(j, 2 * ROWS, stride=2)
            new = adamw(g[1 + j], w_e[rows, :], m_e[rows, :], v_e[rows, :], factor)
            for ref, value in zip((we_o, me_o, ve_o), new):
                ref[rows, :] = value

    gathered = full[0, :, 0:2].reshape(256, WIDE)
    attn_o[...] = jnp.dot(pick[...], gathered, preferred_element_type=F32).astype(BF16)
    exp_o[0] = full[0, :, 2].reshape(128, WIDE)

def comm_part(act_attn, dy_attn, act_exp, dy_exp, w_attn, m_attn, v_attn, w_exp, m_exp, v_exp):
    width = w_attn.shape[1]
    total_params = width * (act_attn.shape[1] + lax.axis_size("expert") * act_exp.shape[2])
    limit = 0.5 * math.sqrt(total_params)
    attn_state = [v.reshape(2 * ROWS, LANES) for v in (w_attn, m_attn, v_attn)]
    exp_state = [
        v.reshape(2, 2 * ROWS, LANES).transpose(1, 0, 2).reshape(4 * ROWS, LANES)
        for v in (w_exp, m_exp, v_exp)
    ]
    hbm = pl.BlockSpec(memory_space=pltpu.HBM)
    n_send = 170

    def blocks(dtype, *lead):
        return pltpu.VMEM(lead + (3, 8, PART), dtype)

    outs = pl.pallas_call(
        lambda *refs: comm_kernel(limit, *refs),
        out_shape=(
            jax.ShapeDtypeStruct((3, 2 * ROWS, LANES), F32),
            jax.ShapeDtypeStruct((8, LANES), F32),
            jax.ShapeDtypeStruct((2, 2, 4, 4, 3, 8, PART), BF16),
        ),
        in_specs=[hbm] * 10,
        out_specs=(hbm,) * 3,
        scratch_shapes=[
            pltpu.VMEM((256, 256), BF16),
            pltpu.VMEM((256, 4 * PART), BF16),
            pltpu.VMEM((128, 128), BF16),
            pltpu.VMEM((128, 4 * PART), BF16),
            *[pltpu.VMEM((2 * ROWS, LANES), F32)] * 3,
            *[pltpu.VMEM((4 * ROWS, LANES), F32)] * 3,
            pltpu.VMEM((3, 2 * ROWS, LANES), F32),
            pltpu.VMEM((8, LANES), F32),
            pltpu.VMEM((256, 256), BF16),
            pltpu.VMEM((128, 128), BF16),
            blocks(BF16, 2, 4, 4),
            blocks(BF16, 2, 4, 4),
            blocks(F32, 2, 4, 4),
            blocks(BF16, 2, 4, 4),
            blocks(BF16, 2, 3, 4),
            blocks(F32, 2),
            blocks(BF16, 2, 3),
            blocks(BF16, 2, 3),
            pltpu.VMEM((16 * ROWS, LANES), F32),
            pltpu.VMEM((8 * ROWS, LANES), F32),
            pltpu.VMEM((16, ROWS, LANES), BF16),
            pltpu.VMEM((4, 2 * ROWS, LANES), BF16),
            pltpu.VMEM((2, 8, ROWS, LANES), BF16),
            pltpu.VMEM((2, 2, 2 * ROWS, LANES), BF16),
            pltpu.VMEM((2, 8, LANES), F32),
            pltpu.VMEM((2, 16, 8, LANES), F32),
            pltpu.VMEM((2, ROWS, LANES), BF16),
            pltpu.VMEM((2, 2 * ROWS, LANES), BF16),
            pltpu.VMEM((16, ROWS, LANES), BF16),
            pltpu.VMEM((4, 2 * ROWS, LANES), BF16),
            pltpu.VMEM((16 * ROWS, LANES), F32),
            pltpu.VMEM((8 * ROWS, LANES), F32),
            blocks(BF16, 2, 4, 4),
            pltpu.SemaphoreType.DMA((n_send,)),
            pltpu.SemaphoreType.DMA((n_send,)),
            pltpu.SemaphoreType.DMA((60,)),
        ],
        compiler_params=pltpu.CompilerParams(
            collective_id=0, has_side_effects=True, vmem_limit_bytes=63 * 1024 * 1024
        ),
    )(act_attn, dy_attn, act_exp, dy_exp, *attn_state, *exp_state)
    return outs, attn_state, exp_state

def body(act_attn, dy_attn, act_exp, dy_exp, *state):
    width = dy_attn.shape[1]
    (g, f, full), attn_state, exp_state = comm_part(act_attn, dy_attn, act_exp, dy_exp, *state)
    steps = width // WIDE
    per_part = PART // WIDE
    whole = lambda shape: pl.BlockSpec(shape, lambda i: (0,) * len(shape))
    a_shape, e_shape = (2 * ROWS, LANES), (4 * ROWS, LANES)
    outs = pl.pallas_call(
        finish_kernel,
        grid=(steps,),
        out_shape=(
            *[jax.ShapeDtypeStruct(a_shape, F32)] * 3,
            *[jax.ShapeDtypeStruct(e_shape, F32)] * 3,
            jax.ShapeDtypeStruct((256, width), BF16),
            jax.ShapeDtypeStruct((1, 128, width), BF16),
        ),
        in_specs=[
            pl.BlockSpec((1, 16, 3, 8, WIDE), lambda i: (i // per_part, 0, 0, 0, i % per_part)),
            whole((3, 2 * ROWS, LANES)),
            whole((8, LANES)),
            *[whole(a_shape)] * 3,
            *[whole(e_shape)] * 3,
        ],
        out_specs=(
            *[whole(a_shape)] * 3,
            *[whole(e_shape)] * 3,
            pl.BlockSpec((256, WIDE), lambda i: (0, i)),
            pl.BlockSpec((1, 128, WIDE), lambda i: (0, 0, i)),
        ),
        scratch_shapes=[pltpu.VMEM((256, 256), BF16)],
        compiler_params=pltpu.CompilerParams(vmem_limit_bytes=63 * 1024 * 1024),
    )(full.reshape(4, 16, 3, 8, PART), g, f, *attn_state, *exp_state)
    attn_new = [v.reshape(1, width) for v in outs[:3]]
    exp_new = [
        v.reshape(2 * ROWS, 2, LANES).transpose(1, 0, 2).reshape(1, 2, width) for v in outs[3:6]
    ]
    return (*attn_new, *exp_new, outs[6], outs[7])

def solution(mesh):
    rows = P(("expert", "dp"), None)
    owned = P("expert", "dp", None)
    return jax.shard_map(
        body,
        mesh=mesh,
        in_specs=(rows, rows, owned, owned, rows, rows, rows, owned, owned, owned),
        out_specs=(rows, rows, rows, owned, owned, owned, P(), P("expert", None, None)),
        check_vma=False,
    )
```

time: 113 us -> 87.7 us (0.78)
  Pallas kernels: 101 us -> 86.8 us
  local copies, waits for them, and re-layouts: 10 us -> 0 us
    pallas_call x1, Pallas kernels: 91.7 us -> 79.2 us  [comm_part(): pl.pallas_call(lambda *refs: comm_kernel(limit, *refs), out_shape=(jax.Sh...]
    unnamed x24 -> x0, local copies, waits for them, and re-layouts: 10 us -> none
    pallas_call x1, Pallas kernels: 9.6 us -> 7.65 us  [body(): pl.pallas_call(finish_kernel, grid=(steps,), out_shape=(*[jax.ShapeDtypeS...]
where the time goes in v2:
time: 87.7 us; the launch traced here: 87.5 us
  Pallas kernels  86.8 us (99%)
    pallas_call x1, Pallas kernels, comm_part(): pl.pallas_call(lambda *refs: comm_kernel(limit, *refs), out_shape=(jax.Sh...  79.2 us
    pallas_call x1, Pallas kernels, body(): pl.pallas_call(finish_kernel, grid=(steps,), out_shape=(*[jax.ShapeDtypeS...  7.65 us

profile of v2, /device:TPU:1, one launch (start us, length us, event | category | flops | bytes accessed | tf_op | source)
XLA Modules:
  0.0 87.5 jit_solution(16433284010970566005)
XLA Ops:
  0.6 79.2 %shard_map.161 = (f32[3,48,128]{2,1,0:T(8,128)}, f32[8,128]{1,0:T(8,128)}, bf16[2,2,4,4,3,8,1536]{6,5,4,3,2,1,0:T(8,128)(2,1)}) custom-call(bf16[256,256]{1,0:T(8,128)(2,1)} %refs_0_.1, bf16[256,6144]{1,0:T(8,128)(2,1)} %refs_1_.1, bf16[1,128,128]{2,1,0:T(8,128)(2,1)} %refs_2_.1, bf16[1,128,6144]{2,1,0:T(8,128)(2,1)} %refs_3_.1, f32[48,128]{1,0:T(8,128)} %bitcast.44, ...), custom_call_target="tpu_custom_call" | custom-call | tf_op jit(solution)/shard_map/pallas_call | solution.py:411
  79.8 7.7 %shard_map.162 = (f32[48,128]{1,0:T(8,128)}, f32[48,128]{1,0:T(8,128)}, f32[48,128]{1,0:T(8,128)}, f32[96,128]{1,0:T(8,128)}, f32[96,128]{1,0:T(8,128)}, /*index...) custom-call(bf16[4,16,3,8,1536]{4,3,2,1,0:T(8,128)(2,1)} %bitcast.37, ...), custom_call_target="tpu_custom_call" | custom-call | tf_op jit(solution)/shard_map/pallas_call | solution.py:471

commit v3 on v2

v3 whole, which is shorter than its diff:
```python
import math

import jax
import jax.numpy as jnp
from jax import lax
from jax.experimental import pallas as pl
from jax.experimental.pallas import tpu as pltpu
from jax.sharding import PartitionSpec as P

beta_first = 0.9
beta_second = 0.95
bias_first = 1.0 - 0.9**10
bias_second = 1.0 - 0.95**10
learn_rate = 0.01
decay_rate = 0.1
adam_eps = 1e-08

MESH = pl.DeviceIdType.MESH
F32 = jnp.float32
BF16 = jnp.bfloat16
HALF = 3072
PART = 1536
LANES = 128
ROWS = HALF // LANES
PROWS = PART // LANES
SUB = 768
SROWS = SUB // LANES
WIDE = 768


def adamw(grad, weight, moment, second, factor):
    scaled = factor * grad
    moment_new = beta_first * moment + (1.0 - beta_first) * scaled
    second_new = beta_second * second + (1.0 - beta_second) * scaled * scaled
    update = moment_new / bias_first / (jnp.sqrt(second_new / bias_second) + adam_eps)
    weight_new = weight - learn_rate * (update + decay_rate * weight)
    return (weight_new, moment_new, second_new)


def grouped(row):
    low = row & 3
    x = (row >> 2) & 3
    y = (row >> 4) & 3
    z_lo = row >> 6
    return ((y * 4 + x) * 4 + z_lo) * 4 + low


def device_at(z, y, x, core):
    return (lax.rem(z, 4), ((y * 4 + x) * 2 + lax.div(z, 4)) * 2 + core)


def aligned(index, multiple):
    return pl.multiple_of(index, multiple)


def comm_kernel(
    limit,
    act_a_hbm, dy_a_hbm, act_e_hbm, dy_e_hbm, w_a_hbm, m_a_hbm, v_a_hbm, w_e_hbm, m_e_hbm, v_e_hbm,
    g_hbm, f_hbm, full,
    act_a, dy_a, act_e, dy_e, w_e, m_e, v_e, g_out, f_out,
    lhs_a, lhs_e, st_a, st_e, pf_a, pf_e,
    cs, cr, own, s1, r1, own2, s2, r2,
    s3_a, s3_e, z3_a, z3_e, r3_a, r3_e,
    n_s, n_r,
    ws_a, ws_e, gr_a, gr_e, g3_a, g3_e, gt,
    send_sem, recv_sem, local_sem,
):
    z_lo = lax.axis_index("expert")
    dp = lax.axis_index("dp")
    core = lax.rem(dp, 2)
    z_hi = lax.rem(lax.div(dp, 2), 2)
    x = lax.rem(lax.div(dp, 4), 4)
    y = lax.div(dp, 16)
    z = z_hi * 4 + z_lo
    other = 1 - core
    peer = device_at(z, y, x, other)

    def zc_mate(dz, dc):
        oz = lax.rem(z + dz, 8)
        oc = core if dc == 0 else other
        return oz, oc

    def plane_mate(dy, dx):
        return device_at(z, lax.rem(y + dy, 4), lax.rem(x + dx, 4), core)

    def axis_mate(axis, d):
        return plane_mate(d, 0) if axis == 0 else plane_mate(0, d)

    place = (y, x)

    kept = []
    waited = []

    def keep(src, dst):
        copy = pltpu.make_async_copy(src, dst, local_sem.at[len(kept)])
        copy.start()
        kept.append(copy)
        return copy

    def need(copies):
        for copy in copies:
            copy.wait()
            waited.append(copy)

    sent = []
    arrived = []

    def send(src, dst, where):
        i = len(sent)
        copy = pltpu.make_async_remote_copy(
            src_ref=src, dst_ref=dst, send_sem=send_sem.at[i], recv_sem=recv_sem.at[i],
            device_id=where, device_id_type=MESH,
        )
        copy.start()
        sent.append(copy)
        return copy

    def arrive(copies):
        for copy in copies:
            copy.wait_recv()
            arrived.append(copy)

    def finish_all():
        arrive([copy for copy in sent if not any(copy is done for done in arrived)])
        for copy in [copy for copy in kept if not any(copy is done for done in waited)]:
            copy.wait()
        for copy in sent:
            copy.wait_send()

    need_act = (keep(act_a_hbm, act_a), keep(act_e_hbm.at[0], act_e))
    need_dy = {}
    for half in range(2):
        for s in range(4):
            cols = pl.ds(aligned((other if half == 0 else core) * HALF + s * SUB, SUB), SUB)
            need_dy[half, s] = (
                keep(dy_a_hbm.at[:, cols], dy_a.at[:, cols]),
                keep(dy_e_hbm.at[0, :, cols], dy_e.at[:, cols]),
            )
    need_state = [
        keep(src, st_a.at[:, pl.ds(k * ROWS, ROWS)]) for k, src in enumerate((w_a_hbm, m_a_hbm, v_a_hbm))
    ] + [keep(src, dst) for src, dst in ((w_e_hbm, w_e), (m_e_hbm, m_e), (v_e_hbm, v_e))]

    barrier = pltpu.get_barrier_semaphore()
    greeted = 0
    for dz in range(8):
        for dc in range(2):
            if dz or dc:
                oz, oc = zc_mate(dz, dc)
                pl.semaphore_signal(barrier, inc=1, device_id=device_at(oz, y, x, oc), device_id_type=MESH)
                greeted += 1
    for dy in range(4):
        for dx in range(4):
            if dy or dx:
                pl.semaphore_signal(barrier, inc=1, device_id=plane_mate(dy, dx), device_id_type=MESH)
                greeted += 1

    r0 = lax.broadcasted_iota(jnp.int32, (256, 256), 0)
    r1_ = lax.broadcasted_iota(jnp.int32, (256, 256), 1)
    pick = jnp.where(r0 == grouped(r1_), 1.0, 0.0).astype(BF16)
    need(need_act)
    lhs_a[...] = lax.dot_general(
        pick, act_a[...], (((1,), (1,)), ((), ())), preferred_element_type=F32
    ).astype(BF16)
    e0 = lax.broadcasted_iota(jnp.int32, (128, 128), 0)
    e1 = lax.broadcasted_iota(jnp.int32, (128, 128), 1)
    same = jnp.where(e0 == e1, 1.0, 0.0).astype(BF16)
    lhs_e[...] = lax.dot_general(
        same, act_e[...], (((1,), (1,)), ((), ())), preferred_element_type=F32
    ).astype(BF16)

    def terms(half, s):
        need(need_dy[half, s])
        cols = pl.ds(aligned((other if half == 0 else core) * HALF + s * SUB, SUB), SUB)
        ga = jnp.dot(lhs_a[...], dy_a[:, cols], preferred_element_type=F32)
        ge = jnp.dot(lhs_e[...], dy_e[:, cols], preferred_element_type=F32)
        return ga.reshape(4, 4, 2, 8, SUB), ge.reshape(4, 4, 8, SUB)

    def block(ref, part, second, first):
        return ref.at[part, second, first] if part % 2 == 0 else ref.at[part, first, second]

    order = (2, 1, 3, 0)
    copies_c, copies_1 = {}, {}

    def give(s):
        ga, ge = terms(0, s)
        cs[s, :, :, 0:2] = ga.astype(BF16)
        cs[s, :, :, 2] = ge.astype(BF16)
        if s == 0:
            pl.semaphore_wait(barrier, greeted)
        copies_c[s] = send(cs.at[s], cr.at[s], peer)

    def take(s):
        ga, ge = terms(1, s)
        own[s, :, :, 0:2] = ga
        own[s, :, :, 2] = ge
        arrive([copies_c[s]])
        for b in range(4):
            both = own[s, b] + cr[s, b].astype(F32)
            own[s, b] = both
            s1[s, b] = both.astype(BF16)
        first = 1 - s % 2
        if s < 2:
            copies_1[s] = []
            for e in (2, 1, 3):
                to = lax.rem(place[first] + e, 4)
                src = s1.at[s, :, to] if s % 2 == 0 else s1.at[s, to]
                copies_1[s].append(send(src, r1.at[s, e - 1], axis_mate(first, e)))
        else:
            for d in order:
                at = lax.rem(place[s % 2] + d, 4)
                copies_1[s, d] = [
                    send(
                        block(s1, s, at, lax.rem(place[first] + e, 4)),
                        r1.at[s, e - 1, at],
                        axis_mate(first, e),
                    )
                    for e in (2, 1, 3)
                ]

    give(0)
    z_order = (4, 3, 5, 2, 6, 1, 7, 0)
    my_q = z_lo * 4 + z_hi * 2 + core
    my_e = z_hi * 2 + core
    need(need_state)
    for h in range(2):
        for j in range(2):
            for k, state in enumerate((w_e, m_e, v_e)):
                st_e[h, pl.ds((j * 3 + k) * ROWS, ROWS), :] = state[pl.ds(h * 2 * ROWS + j, ROWS, stride=2), :]
    pf_at_a = pl.ds(aligned(my_q * 3 * ROWS, 8), 3 * ROWS)
    pf_at_e = pl.ds(aligned(my_e * 6 * ROWS, 8), 6 * ROWS)
    copies_pf = []
    for dz in z_order:
        for dc in range(2):
            if dz or dc:
                oz, oc = zc_mate(dz, dc)
                copies_pf.append(send(st_a.at[oc], pf_a.at[pf_at_a], device_at(oz, y, x, oc)))
                if dz in (0, 4):
                    copies_pf.append(send(st_e.at[oc], pf_e.at[pf_at_e], device_at(oz, y, x, oc)))
    pf_a[pf_at_a, :] = st_a[core]
    pf_e[pf_at_e, :] = st_e[core]

    give(1)
    take(0)
    take(1)
    give(2)
    give(3)
    take(2)
    take(3)

    copies_2 = {s: [] for s in range(4)}

    def pass_on(s, d):
        at = lax.rem(place[s % 2] + d, 4)
        total = block(own, s, at, place[1 - s % 2])[...]
        for e in range(3):
            total = total + r1[s, e, at].astype(F32)
        if d:
            s2[s, d - 1] = total.astype(BF16)
            copies_2[s].append(send(s2.at[s, d - 1], r2.at[s, d - 1], axis_mate(s % 2, d)))
        else:
            own2[s] = total

    for s in (0, 1):
        arrive(copies_1[s])
        for d in order:
            pass_on(s, d)
    for d in order:
        for s in (2, 3):
            arrive(copies_1[s, d])
            pass_on(s, d)

    for s in range(4):
        arrive(copies_2[s])
        total = own2[s]
        for d in range(3):
            total = total + r2[s, d].astype(F32)
        total_a = total[0:2].reshape(16, SUB)
        total_e = total[2]
        for t in range(SROWS):
            lanes = slice(t * LANES, (t + 1) * LANES)
            s3_a[pl.ds(s * SROWS + t, 16, stride=ROWS), :] = total_a[:, lanes]
            s3_e[pl.ds(s * SROWS + t, 8, stride=ROWS), :] = total_e[:, lanes]
    z3_a[...] = s3_a[...].astype(BF16).reshape(16, ROWS, LANES)
    z3_e[...] = s3_e[...].astype(BF16).reshape(4, 2 * ROWS, LANES)

    batch = []
    for dz in z_order:
        for dc in range(2):
            if dz or dc:
                oz, oc = zc_mate(dz, dc)
                q = lax.rem(oz, 4) * 4 + lax.div(oz, 4) * 2 + oc
                batch.append(send(z3_a.at[q], r3_a.at[dc, dz], device_at(oz, y, x, oc)))
                if dz in (0, 4):
                    q = lax.div(oz, 4) * 2 + oc
                    batch.append(send(z3_e.at[q], r3_e.at[dc, dz // 4], device_at(oz, y, x, oc)))
    arrive(batch)

    near = s3_a[pl.ds(aligned(my_q * ROWS, 8), ROWS), :]
    far = r3_a[1, 0].astype(F32)
    for dz in range(1, 8):
        near = near + r3_a[0, dz].astype(F32)
        far = far + r3_a[1, dz].astype(F32)
    near_at = pl.ds(aligned(core * ROWS, 8), ROWS)
    far_at = pl.ds(aligned(other * ROWS, 8), ROWS)
    g_out[0, near_at, :] = near
    g_out[0, far_at, :] = far
    near_e = s3_e[pl.ds(aligned(my_e * 2 * ROWS, 8), 2 * ROWS), :] + r3_e[0, 1].astype(F32)
    far_e = r3_e[1, 0].astype(F32) + r3_e[1, 1].astype(F32)
    for j in range(2):
        g_out[1 + j, near_at, :] = near_e[j * ROWS : (j + 1) * ROWS]
        g_out[1 + j, far_at, :] = far_e[j * ROWS : (j + 1) * ROWS]

    square = jnp.zeros((8, LANES), F32)
    for piece in (near, far, near_e, far_e):
        for i in range(piece.shape[0] // 8):
            part_of = piece[i * 8 : (i + 1) * 8]
            square = square + part_of * part_of
    n_s[0] = square
    batch = []
    for dz in z_order:
        for dc in range(2):
            if dz or dc:
                oz, oc = zc_mate(dz, dc)
                batch.append(send(n_s.at[0], n_r.at[0, dz * 2 + dc], device_at(oz, y, x, oc)))
    ws_a[core] = near.astype(BF16)
    ws_a[other] = far.astype(BF16)
    ws_e[core] = near_e.astype(BF16)
    ws_e[other] = far_e.astype(BF16)
    copies_g = []
    for dz in z_order:
        for dc in range(2):
            if dz or dc:
                oz, oc = zc_mate(dz, dc)
                copies_g.append(send(ws_a.at[oc], gr_a.at[my_q], device_at(oz, y, x, oc)))
                if dz in (0, 4):
                    copies_g.append(send(ws_e.at[oc], gr_e.at[my_e], device_at(oz, y, x, oc)))
    gr_a[my_q] = ws_a[core]
    gr_e[my_e] = ws_e[core]
    keep(g_out, g_hbm)
    arrive(batch)
    for i in range(1, 16):
        square = square + n_r[0, i]
    n_s[1] = square
    batch = []
    for dy in order:
        for dx in order:
            if dy or dx:
                batch.append(send(n_s.at[1], n_r.at[1, dy * 4 + dx], plane_mate(dy, dx)))
    arrive(copies_g)
    g3_a[...] = gr_a[...].astype(F32).reshape(16 * ROWS, LANES)
    g3_e[...] = gr_e[...].astype(F32).reshape(8 * ROWS, LANES)
    arrive(copies_pf)
    arrive(batch)
    for i in range(1, 16):
        square = square + n_r[1, i]
    norm = jnp.sqrt(jnp.sum(square, keepdims=True))
    factor = jnp.minimum(1.0, limit / (norm + 1e-06))
    f_out[...] = jnp.broadcast_to(factor, (8, LANES))
    keep(f_out, f_hbm)

    def new_tile(rows, grad, state, t):
        values = [state[pl.ds(k * ROWS + t, rows, stride=3 * ROWS), :] for k in range(3)]
        return adamw(grad[pl.ds(t, rows, stride=ROWS), :], *values, factor)[0].astype(BF16)

    for part in range(2):
        for t in range(PROWS):
            lanes = pl.ds(t * LANES, LANES)
            gt[part, y, x, 0:2, :, lanes] = new_tile(16, g3_a, pf_a, part * PROWS + t).reshape(2, 8, LANES)
            gt[part, y, x, 2, :, lanes] = new_tile(8, g3_e, pf_e, part * PROWS + t)

    def spread(part, at):
        here = block(gt, part, at, place[1 - part])
        return {e: send(here, here, axis_mate(1 - part, e)) for e in (2, 1, 3)}

    def deliver(part, at, first_at):
        src = block(gt, part, at, first_at)
        dst = block(full.at[core], part, at, first_at)
        send(src, dst, peer)
        keep(src, dst)

    copies_2 = [{}, {}]
    for part in range(2):
        here = gt.at[part, y, x]
        copies_2[part] = {d: send(here, here, axis_mate(part, d)) for d in (2, 1, 3)}
    copies_1 = [{0: spread(part, place[part])} for part in range(2)]
    for part in range(2):
        deliver(part, place[part], place[1 - part])
    for d in (1, 3, 2):
        for part in range(2):
            at = lax.rem(place[part] + 4 - d, 4)
            arrive([copies_2[part][d]])
            copies_1[part][d] = spread(part, at)
            deliver(part, at, place[1 - part])
    for d in (0, 1, 3, 2):
        for part in range(2):
            at = lax.rem(place[part] + 4 - d, 4)
            for e in (1, 3, 2):
                arrive([copies_1[part][d][e]])
                deliver(part, at, lax.rem(place[1 - part] + 4 - e, 4))
    finish_all()


def finish_kernel(
    full, g_hbm, f_hbm, w_a_hbm, m_a_hbm, v_a_hbm, w_e_hbm, m_e_hbm, v_e_hbm,
    wa_o, ma_o, va_o, we_o, me_o, ve_o, attn_o, exp_o,
    got, attn, g, f, st_a, st_e, new_a, new_e, pick, in_sem, out_sem, small_sem,
):
    reads = []
    for i in range(2 * HALF // WIDE):
        half, at = divmod(i * WIDE, PART)
        reads.append(pltpu.make_async_copy(full.at[half, :, :, :, pl.ds(at, WIDE)], got.at[i], in_sem.at[i]))
    pairs = [(g_hbm, g), (f_hbm, f)]
    pairs += [(ref, st_a.at[k]) for k, ref in enumerate((w_a_hbm, m_a_hbm, v_a_hbm))]
    pairs += [(ref, st_e.at[k]) for k, ref in enumerate((w_e_hbm, m_e_hbm, v_e_hbm))]
    small = [pltpu.make_async_copy(src, dst, small_sem.at[k]) for k, (src, dst) in enumerate(pairs)]
    for copy in reads[:2] + small + reads[2:]:
        copy.start()
    r0 = lax.broadcasted_iota(jnp.int32, (256, 256), 0)
    r1 = lax.broadcasted_iota(jnp.int32, (256, 256), 1)
    pick[...] = jnp.where(grouped(r0) == r1, 1.0, 0.0).astype(BF16)

    writes = []

    def write(src, dst):
        copy = pltpu.make_async_copy(src, dst, out_sem.at[len(writes)])
        copy.start()
        writes.append(copy)

    for i, copy in enumerate(reads):
        copy.wait()
        cols = pl.ds(i * WIDE, WIDE)
        write(got.at[i, :, 2], exp_o.at[:, :, cols])
        gathered = got[i, :, 0:2].reshape(256, WIDE)
        attn[i] = jnp.dot(pick[...], gathered, preferred_element_type=F32).astype(BF16)
        write(attn.at[i], attn_o.at[:, cols])
        if i == 1:
            for one in small:
                one.wait()
            factor = f[0:1, 0:1]
            new = adamw(g[0], st_a[0], st_a[1], st_a[2], factor)
            for k, ref in enumerate((wa_o, ma_o, va_o)):
                new_a[k] = new[k]
                write(new_a.at[k], ref)
            for j in range(2):
                rows = pl.ds(j, 2 * ROWS, stride=2)
                new = adamw(g[1 + j], *[st_e[k, rows, :] for k in range(3)], factor)
                for k in range(3):
                    new_e[k, rows, :] = new[k]
            for k, ref in enumerate((we_o, me_o, ve_o)):
                write(new_e.at[k], ref)
    for copy in writes:
        copy.wait()


def comm_part(act_attn, dy_attn, act_exp, dy_exp, w_attn, m_attn, v_attn, w_exp, m_exp, v_exp):
    width = w_attn.shape[1]
    total_params = width * (act_attn.shape[1] + lax.axis_size("expert") * act_exp.shape[2])
    limit = 0.5 * math.sqrt(total_params)
    attn_state = [v.reshape(2, ROWS, LANES) for v in (w_attn, m_attn, v_attn)]
    exp_state = [
        v.reshape(2, 2 * ROWS, LANES).transpose(1, 0, 2).reshape(4 * ROWS, LANES)
        for v in (w_exp, m_exp, v_exp)
    ]
    hbm = pl.BlockSpec(memory_space=pltpu.HBM)
    n_send = 200

    def blocks(dtype, *lead, width=SUB):
        return pltpu.VMEM(lead + (3, 8, width), dtype)

    outs = pl.pallas_call(
        lambda *refs: comm_kernel(limit, *refs),
        out_shape=(
            jax.ShapeDtypeStruct((3, 2 * ROWS, LANES), F32),
            jax.ShapeDtypeStruct((8, LANES), F32),
            jax.ShapeDtypeStruct((2, 2, 4, 4, 3, 8, PART), BF16),
        ),
        in_specs=[hbm] * 10,
        out_specs=(hbm,) * 3,
        scratch_shapes=[
            pltpu.VMEM((256, 256), BF16),
            pltpu.VMEM((256, 4 * PART), BF16),
            pltpu.VMEM((128, 128), BF16),
            pltpu.VMEM((128, 4 * PART), BF16),
            *[pltpu.VMEM((4 * ROWS, LANES), F32)] * 3,
            pltpu.VMEM((3, 2 * ROWS, LANES), F32),
            pltpu.VMEM((8, LANES), F32),
            pltpu.VMEM((256, 256), BF16),
            pltpu.VMEM((128, 128), BF16),
            pltpu.VMEM((2, 3 * ROWS, LANES), F32),
            pltpu.VMEM((2, 6 * ROWS, LANES), F32),
            pltpu.VMEM((16 * 3 * ROWS, LANES), F32),
            pltpu.VMEM((8 * 3 * ROWS, LANES), F32),
            blocks(BF16, 4, 4, 4),
            blocks(BF16, 4, 4, 4),
            blocks(F32, 4, 4, 4),
            blocks(BF16, 4, 4, 4),
            blocks(BF16, 4, 3, 4),
            blocks(F32, 4),
            blocks(BF16, 4, 3),
            blocks(BF16, 4, 3),
            pltpu.VMEM((16 * ROWS, LANES), F32),
            pltpu.VMEM((8 * ROWS, LANES), F32),
            pltpu.VMEM((16, ROWS, LANES), BF16),
            pltpu.VMEM((4, 2 * ROWS, LANES), BF16),
            pltpu.VMEM((2, 8, ROWS, LANES), BF16),
            pltpu.VMEM((2, 2, 2 * ROWS, LANES), BF16),
            pltpu.VMEM((2, 8, LANES), F32),
            pltpu.VMEM((2, 16, 8, LANES), F32),
            pltpu.VMEM((2, ROWS, LANES), BF16),
            pltpu.VMEM((2, 2 * ROWS, LANES), BF16),
            pltpu.VMEM((16, ROWS, LANES), BF16),
            pltpu.VMEM((4, 2 * ROWS, LANES), BF16),
            pltpu.VMEM((16 * ROWS, LANES), F32),
            pltpu.VMEM((8 * ROWS, LANES), F32),
            blocks(BF16, 2, 4, 4, width=PART),
            pltpu.SemaphoreType.DMA((n_send,)),
            pltpu.SemaphoreType.DMA((n_send,)),
            pltpu.SemaphoreType.DMA((80,)),
        ],
        compiler_params=pltpu.CompilerParams(
            collective_id=0, has_side_effects=True, vmem_limit_bytes=63 * 1024 * 1024
        ),
    )(act_attn, dy_attn, act_exp, dy_exp, *attn_state, *exp_state)
    return outs, attn_state, exp_state


def body(act_attn, dy_attn, act_exp, dy_exp, *state):
    width = dy_attn.shape[1]
    (g, f, full), attn_state, exp_state = comm_part(act_attn, dy_attn, act_exp, dy_exp, *state)
    a_shape, e_shape = (2 * ROWS, LANES), (4 * ROWS, LANES)
    steps = width // WIDE
    hbm = pl.BlockSpec(memory_space=pltpu.HBM)
    outs = pl.pallas_call(
        finish_kernel,
        out_shape=(
            *[jax.ShapeDtypeStruct(a_shape, F32)] * 3,
            *[jax.ShapeDtypeStruct(e_shape, F32)] * 3,
            jax.ShapeDtypeStruct((256, width), BF16),
            jax.ShapeDtypeStruct((16, 8, width), BF16),
        ),
        in_specs=[hbm] * 9,
        out_specs=(hbm,) * 8,
        scratch_shapes=[
            pltpu.VMEM((steps, 16, 3, 8, WIDE), BF16),
            pltpu.VMEM((steps, 256, WIDE), BF16),
            pltpu.VMEM((3, 2 * ROWS, LANES), F32),
            pltpu.VMEM((8, LANES), F32),
            pltpu.VMEM((3,) + a_shape, F32),
            pltpu.VMEM((3,) + e_shape, F32),
            pltpu.VMEM((3,) + a_shape, F32),
            pltpu.VMEM((3,) + e_shape, F32),
            pltpu.VMEM((256, 256), BF16),
            pltpu.SemaphoreType.DMA((steps,)),
            pltpu.SemaphoreType.DMA((2 * steps + 6,)),
            pltpu.SemaphoreType.DMA((8,)),
        ],
        compiler_params=pltpu.CompilerParams(vmem_limit_bytes=63 * 1024 * 1024),
    )(full.reshape(4, 16, 3, 8, PART), g, f, *[v.reshape(a_shape) for v in attn_state], *exp_state)
    attn_new = [v.reshape(1, width) for v in outs[:3]]
    exp_new = [
        v.reshape(2 * ROWS, 2, LANES).transpose(1, 0, 2).reshape(1, 2, width) for v in outs[3:6]
    ]
    return (*attn_new, *exp_new, outs[6], outs[7].reshape(1, 128, width))


def solution(mesh):
    rows = P(("expert", "dp"), None)
    owned = P("expert", "dp", None)
    return jax.shard_map(
        body,
        mesh=mesh,
        in_specs=(rows, rows, owned, owned, rows, rows, rows, owned, owned, owned),
        out_specs=(rows, rows, rows, owned, owned, owned, P(), P("expert", None, None)),
        check_vma=False,
    )
```

time: 87.7 us -> 78.5 us (0.90)
  Pallas kernels: 86.8 us -> 77.8 us
    pallas_call x1, Pallas kernels: 79.2 us -> 72.5 us  [comm_part(): pl.pallas_call(lambda *refs: comm_kernel(limit, *refs), out_shape=(jax.Sh...]
    pallas_call x1, Pallas kernels: 7.65 us -> 5.27 us  [body(): pl.pallas_call(finish_kernel, out_shape=(*[jax.ShapeDtypeStruct(a_shape,...]
where the time goes in v3:
time: 78.5 us; the launch traced here: 78.4 us
  Pallas kernels  77.8 us (99%)
    pallas_call x1, Pallas kernels, comm_part(): pl.pallas_call(lambda *refs: comm_kernel(limit, *refs), out_shape=(jax.Sh...  72.5 us
    pallas_call x1, Pallas kernels, body(): pl.pallas_call(finish_kernel, out_shape=(*[jax.ShapeDtypeStruct(a_shape,...  5.27 us

profile of v3, /device:TPU:1, one launch (start us, length us, event | category | flops | bytes accessed | tf_op | source)
XLA Modules:
  0.0 78.4 jit_solution(10098491036162154703)
XLA Ops:
  0.6 72.5 %shard_map.161 = (f32[3,48,128]{2,1,0:T(8,128)}, f32[8,128]{1,0:T(8,128)}, bf16[2,2,4,4,3,8,1536]{6,5,4,3,2,1,0:T(8,128)(2,1)}) custom-call(bf16[256,256]{1,0:T(8,128)(2,1)} %refs_0_.1, bf16[256,6144]{1,0:T(8,128)(2,1)} %refs_1_.1, bf16[1,128,128]{2,1,0:T(8,128)(2,1)} %refs_2_.1, bf16[1,128,6144]{2,1,0:T(8,128)(2,1)} %refs_3_.1, f32[2,24,128]{2,1,0:T(8,128)} %bitcast.48, ...), custom_call_target="tpu_custom_call" | custom-call | tf_op jit(solution)/shard_map/pallas_call | solution.py:470
  73.2 5.3 %shard_map.162 = (f32[48,128]{1,0:T(8,128)}, f32[48,128]{1,0:T(8,128)}, f32[48,128]{1,0:T(8,128)}, f32[96,128]{1,0:T(8,128)}, f32[96,128]{1,0:T(8,128)}, /*index...) custom-call(bf16[4,16,3,8,1536]{4,3,2,1,0:T(8,128)(2,1)} %bitcast.41, ...), custom_call_target="tpu_custom_call" | custom-call | tf_op jit(solution)/shard_map/pallas_call | solution.py:533

commit v4 on v3

--- a/solution.py
+++ b/solution.py
@@ -25,7 +25,6 @@
 PROWS = PART // LANES
 SUB = 768
 SROWS = SUB // LANES
-WIDE = 768
 
 
 def adamw(grad, weight, moment, second, factor):
@@ -56,13 +55,13 @@
 def comm_kernel(
     limit,
     act_a_hbm, dy_a_hbm, act_e_hbm, dy_e_hbm, w_a_hbm, m_a_hbm, v_a_hbm, w_e_hbm, m_e_hbm, v_e_hbm,
-    g_hbm, f_hbm, full,
-    act_a, dy_a, act_e, dy_e, w_e, m_e, v_e, g_out, f_out,
+    g_out, f_out, full_a, full_e,
+    act_a, dy_a, act_e, dy_e, w_e, m_e, v_e,
     lhs_a, lhs_e, st_a, st_e, pf_a, pf_e,
     cs, cr, own, s1, r1, own2, s2, r2,
     s3_a, s3_e, z3_a, z3_e, r3_a, r3_e,
     n_s, n_r,
-    ws_a, ws_e, gr_a, gr_e, g3_a, g3_e, gt,
+    ws_a, ws_e, gr_a, gr_e, g3_a, g3_e,
     send_sem, recv_sem, local_sem,
 ):
     z_lo = lax.axis_index("expert")
@@ -175,7 +174,7 @@
         ge = jnp.dot(lhs_e[...], dy_e[:, cols], preferred_element_type=F32)
         return ga.reshape(4, 4, 2, 8, SUB), ge.reshape(4, 4, 8, SUB)
 
-    def block(ref, part, second, first):
+    def piece(ref, part, second, first):
         return ref.at[part, second, first] if part % 2 == 0 else ref.at[part, first, second]
 
     order = (2, 1, 3, 0)
@@ -210,7 +209,7 @@
                 at = lax.rem(place[s % 2] + d, 4)
                 copies_1[s, d] = [
                     send(
-                        block(s1, s, at, lax.rem(place[first] + e, 4)),
+                        piece(s1, s, at, lax.rem(place[first] + e, 4)),
                         r1.at[s, e - 1, at],
                         axis_mate(first, e),
                     )
@@ -251,7 +250,7 @@
 
     def pass_on(s, d):
         at = lax.rem(place[s % 2] + d, 4)
-        total = block(own, s, at, place[1 - s % 2])[...]
+        total = piece(own, s, at, place[1 - s % 2])[...]
         for e in range(3):
             total = total + r1[s, e, at].astype(F32)
         if d:
@@ -336,7 +335,6 @@
                     copies_g.append(send(ws_e.at[oc], gr_e.at[my_e], device_at(oz, y, x, oc)))
     gr_a[my_q] = ws_a[core]
     gr_e[my_e] = ws_e[core]
-    keep(g_out, g_hbm)
     arrive(batch)
     for i in range(1, 16):
         square = square + n_r[0, i]
@@ -356,65 +354,84 @@
     norm = jnp.sqrt(jnp.sum(square, keepdims=True))
     factor = jnp.minimum(1.0, limit / (norm + 1e-06))
     f_out[...] = jnp.broadcast_to(factor, (8, LANES))
-    keep(f_out, f_hbm)
 
     def new_tile(rows, grad, state, t):
         values = [state[pl.ds(k * ROWS + t, rows, stride=3 * ROWS), :] for k in range(3)]
         return adamw(grad[pl.ds(t, rows, stride=ROWS), :], *values, factor)[0].astype(BF16)
 
+    even = 2 * lax.rem(lax.div(z_lo + 1, 2), 2)
+    odd = 2 * lax.div(z_lo, 2) + 1
+    mine = (even, odd)
+    swapped = (2 - even, 4 - odd)
+    swap_z = (lax.rem(z + 1 + 6 * lax.rem(z, 2), 8), lax.rem(z + 7 - 6 * lax.rem(z, 2), 8))
+
+    def spread(ref, lead, part, at):
+        here = block(ref, lead, part, at, place[1 - part])
+        return [send(here, here, axis_mate(1 - part, e)) for e in (2, 1, 3)]
+
+    def block(ref, lead, part, second, first):
+        return ref.at[lead, second, first] if part == 0 else ref.at[lead, first, second]
+
+    def strip(ref, lead, part, second):
+        return ref.at[lead, second] if part == 0 else ref.at[lead, :, second]
+
+    def deliver(ref, lead, part, second):
+        src = strip(ref, lead, part, second)
+        send(src, src, peer)
+
+    gt_a = full_a.at[core]
+    gt_e = full_e.at[core]
+    first_a, second_a, first_e, second_e = {}, {}, {}, {}
+    for part in range(2):
+        for t in range(SROWS):
+            tile = new_tile(16, g3_a, pf_a, mine[part] * SROWS + t)
+            gt_a[mine[part], y, x, :, :, pl.ds(t * LANES, LANES)] = tile.reshape(2, 8, LANES)
+        here = gt_a.at[mine[part], y, x]
+        for d in (2, 1, 3):
+            second_a[part, d] = send(here, here, axis_mate(part, d))
+        first_a[part, 0] = spread(gt_a, mine[part], part, place[part])
     for part in range(2):
         for t in range(PROWS):
-            lanes = pl.ds(t * LANES, LANES)
-            gt[part, y, x, 0:2, :, lanes] = new_tile(16, g3_a, pf_a, part * PROWS + t).reshape(2, 8, LANES)
-            gt[part, y, x, 2, :, lanes] = new_tile(8, g3_e, pf_e, part * PROWS + t)
-
-    def spread(part, at):
-        here = block(gt, part, at, place[1 - part])
-        return {e: send(here, here, axis_mate(1 - part, e)) for e in (2, 1, 3)}
-
-    def deliver(part, at, first_at):
-        src = block(gt, part, at, first_at)
-        dst = block(full.at[core], part, at, first_at)
-        send(src, dst, peer)
-        keep(src, dst)
-
-    copies_2 = [{}, {}]
-    for part in range(2):
-        here = gt.at[part, y, x]
-        copies_2[part] = {d: send(here, here, axis_mate(part, d)) for d in (2, 1, 3)}
-    copies_1 = [{0: spread(part, place[part])} for part in range(2)]
-    for part in range(2):
-        deliver(part, place[part], place[1 - part])
+            gt_e[part, y, x, :, pl.ds(t * LANES, LANES)] = new_tile(8, g3_e, pf_e, part * PROWS + t)
+        here = gt_e.at[part, y, x]
+        for d in (2, 1, 3):
+            second_e[part, d] = send(here, here, axis_mate(part, d))
+        first_e[part, 0] = spread(gt_e, part, part, place[part])
+
+    def from_mate(part, d):
+        return lax.rem(place[part] + 4 - d, 4)
+
     for d in (1, 3, 2):
         for part in range(2):
-            at = lax.rem(place[part] + 4 - d, 4)
-            arrive([copies_2[part][d]])
-            copies_1[part][d] = spread(part, at)
-            deliver(part, at, place[1 - part])
+            arrive([second_a[part, d]])
+            first_a[part, d] = spread(gt_a, mine[part], part, from_mate(part, d))
+    for d in (1, 3, 2):
+        for part in range(2):
+            arrive([second_e[part, d]])
+            first_e[part, d] = spread(gt_e, part, part, from_mate(part, d))
+    swaps = {}
     for d in (0, 1, 3, 2):
         for part in range(2):
-            at = lax.rem(place[part] + 4 - d, 4)
-            for e in (1, 3, 2):
-                arrive([copies_1[part][d][e]])
-                deliver(part, at, lax.rem(place[1 - part] + 4 - e, 4))
+            at = from_mate(part, d)
+            arrive(first_a[part, d])
+            ready = strip(gt_a, mine[part], part, at)
+            swaps[part, d] = send(ready, ready, device_at(swap_z[part], y, x, core))
+            deliver(gt_a, mine[part], part, at)
+    for d in (0, 1, 3, 2):
+        for part in range(2):
+            at = from_mate(part, d)
+            arrive(first_e[part, d])
+            deliver(gt_e, part, part, at)
+            arrive([swaps[part, d]])
+            deliver(gt_a, swapped[part], part, at)
     finish_all()
 
 
 def finish_kernel(
-    full, g_hbm, f_hbm, w_a_hbm, m_a_hbm, v_a_hbm, w_e_hbm, m_e_hbm, v_e_hbm,
+    full_a, full_e, g, f, w_a, m_a, v_a, w_e, m_e, v_e,
     wa_o, ma_o, va_o, we_o, me_o, ve_o, attn_o, exp_o,
-    got, attn, g, f, st_a, st_e, new_a, new_e, pick, in_sem, out_sem, small_sem,
+    attn, new_a, new_e, pick, out_sem,
 ):
-    reads = []
-    for i in range(2 * HALF // WIDE):
-        half, at = divmod(i * WIDE, PART)
-        reads.append(pltpu.make_async_copy(full.at[half, :, :, :, pl.ds(at, WIDE)], got.at[i], in_sem.at[i]))
-    pairs = [(g_hbm, g), (f_hbm, f)]
-    pairs += [(ref, st_a.at[k]) for k, ref in enumerate((w_a_hbm, m_a_hbm, v_a_hbm))]
-    pairs += [(ref, st_e.at[k]) for k, ref in enumerate((w_e_hbm, m_e_hbm, v_e_hbm))]
-    small = [pltpu.make_async_copy(src, dst, small_sem.at[k]) for k, (src, dst) in enumerate(pairs)]
-    for copy in reads[:2] + small + reads[2:]:
-        copy.start()
     r0 = lax.broadcasted_iota(jnp.int32, (256, 256), 0)
     r1 = lax.broadcasted_iota(jnp.int32, (256, 256), 1)
     pick[...] = jnp.where(grouped(r0) == r1, 1.0, 0.0).astype(BF16)
@@ -426,28 +443,24 @@
         copy.start()
         writes.append(copy)
 
-    for i, copy in enumerate(reads):
-        copy.wait()
-        cols = pl.ds(i * WIDE, WIDE)
-        write(got.at[i, :, 2], exp_o.at[:, :, cols])
-        gathered = got[i, :, 0:2].reshape(256, WIDE)
+    for i in range(2 * HALF // PART):
+        write(full_e.at[i], exp_o.at[:, :, pl.ds(i * PART, PART)])
+    for i in range(2 * HALF // SUB):
+        gathered = full_a[i].reshape(256, SUB)
         attn[i] = jnp.dot(pick[...], gathered, preferred_element_type=F32).astype(BF16)
-        write(attn.at[i], attn_o.at[:, cols])
-        if i == 1:
-            for one in small:
-                one.wait()
-            factor = f[0:1, 0:1]
-            new = adamw(g[0], st_a[0], st_a[1], st_a[2], factor)
-            for k, ref in enumerate((wa_o, ma_o, va_o)):
-                new_a[k] = new[k]
-                write(new_a.at[k], ref)
-            for j in range(2):
-                rows = pl.ds(j, 2 * ROWS, stride=2)
-                new = adamw(g[1 + j], *[st_e[k, rows, :] for k in range(3)], factor)
-                for k in range(3):
-                    new_e[k, rows, :] = new[k]
-            for k, ref in enumerate((we_o, me_o, ve_o)):
-                write(new_e.at[k], ref)
+        write(attn.at[i], attn_o.at[:, pl.ds(i * SUB, SUB)])
+    factor = f[0:1, 0:1]
+    new = adamw(g[0], w_a[...], m_a[...], v_a[...], factor)
+    for k, ref in enumerate((wa_o, ma_o, va_o)):
+        new_a[k] = new[k]
+        write(new_a.at[k], ref)
+    for j in range(2):
+        rows = pl.ds(j, 2 * ROWS, stride=2)
+        new = adamw(g[1 + j], w_e[rows, :], m_e[rows, :], v_e[rows, :], factor)
+        for k in range(3):
+            new_e[k, rows, :] = new[k]
+    for k, ref in enumerate((we_o, me_o, ve_o)):
+        write(new_e.at[k], ref)
     for copy in writes:
         copy.wait()
 
@@ -462,28 +475,28 @@
         for v in (w_exp, m_exp, v_exp)
     ]
     hbm = pl.BlockSpec(memory_space=pltpu.HBM)
-    n_send = 200
-
-    def blocks(dtype, *lead, width=SUB):
-        return pltpu.VMEM(lead + (3, 8, width), dtype)
+    vmem = pl.BlockSpec(memory_space=pltpu.VMEM)
+    n_send = 230
+
+    def blocks(dtype, *lead):
+        return pltpu.VMEM(lead + (3, 8, SUB), dtype)
 
     outs = pl.pallas_call(
         lambda *refs: comm_kernel(limit, *refs),
         out_shape=(
             jax.ShapeDtypeStruct((3, 2 * ROWS, LANES), F32),
             jax.ShapeDtypeStruct((8, LANES), F32),
-            jax.ShapeDtypeStruct((2, 2, 4, 4, 3, 8, PART), BF16),
+            jax.ShapeDtypeStruct((2, 4, 4, 4, 2, 8, SUB), BF16),
+            jax.ShapeDtypeStruct((2, 2, 4, 4, 8, PART), BF16),
         ),
         in_specs=[hbm] * 10,
-        out_specs=(hbm,) * 3,
+        out_specs=(vmem,) * 4,
         scratch_shapes=[
             pltpu.VMEM((256, 256), BF16),
             pltpu.VMEM((256, 4 * PART), BF16),
             pltpu.VMEM((128, 128), BF16),
             pltpu.VMEM((128, 4 * PART), BF16),
             *[pltpu.VMEM((4 * ROWS, LANES), F32)] * 3,
-            pltpu.VMEM((3, 2 * ROWS, LANES), F32),
-            pltpu.VMEM((8, LANES), F32),
             pltpu.VMEM((256, 256), BF16),
             pltpu.VMEM((128, 128), BF16),
             pltpu.VMEM((2, 3 * ROWS, LANES), F32),
@@ -512,24 +525,24 @@
             pltpu.VMEM((4, 2 * ROWS, LANES), BF16),
             pltpu.VMEM((16 * ROWS, LANES), F32),
             pltpu.VMEM((8 * ROWS, LANES), F32),
-            blocks(BF16, 2, 4, 4, width=PART),
             pltpu.SemaphoreType.DMA((n_send,)),
             pltpu.SemaphoreType.DMA((n_send,)),
             pltpu.SemaphoreType.DMA((80,)),
         ],
         compiler_params=pltpu.CompilerParams(
-            collective_id=0, has_side_effects=True, vmem_limit_bytes=63 * 1024 * 1024
+            collective_id=0, has_side_effects=True, vmem_limit_bytes=36 * 1024 * 1024
         ),
-    )(act_attn, dy_attn, act_exp, dy_exp, *attn_state, *exp_state)
+    )(*[pltpu.with_memory_space_constraint(v, pltpu.HBM) for v in (act_attn, dy_attn, act_exp, dy_exp, *attn_state, *exp_state)])
     return outs, attn_state, exp_state
 
 
 def body(act_attn, dy_attn, act_exp, dy_exp, *state):
     width = dy_attn.shape[1]
-    (g, f, full), attn_state, exp_state = comm_part(act_attn, dy_attn, act_exp, dy_exp, *state)
+    (g, f, full_a, full_e), attn_state, exp_state = comm_part(act_attn, dy_attn, act_exp, dy_exp, *state)
     a_shape, e_shape = (2 * ROWS, LANES), (4 * ROWS, LANES)
-    steps = width // WIDE
+    steps = width // SUB
     hbm = pl.BlockSpec(memory_space=pltpu.HBM)
+    vmem = pl.BlockSpec(memory_space=pltpu.VMEM)
     outs = pl.pallas_call(
         finish_kernel,
         out_shape=(
@@ -538,24 +551,17 @@
             jax.ShapeDtypeStruct((256, width), BF16),
             jax.ShapeDtypeStruct((16, 8, width), BF16),
         ),
-        in_specs=[hbm] * 9,
+        in_specs=[vmem] * 10,
         out_specs=(hbm,) * 8,
         scratch_shapes=[
-            pltpu.VMEM((steps, 16, 3, 8, WIDE), BF16),
-            pltpu.VMEM((steps, 256, WIDE), BF16),
-            pltpu.VMEM((3, 2 * ROWS, LANES), F32),
-            pltpu.VMEM((8, LANES), F32),
-            pltpu.VMEM((3,) + a_shape, F32),
-            pltpu.VMEM((3,) + e_shape, F32),
+            pltpu.VMEM((steps, 256, SUB), BF16),
             pltpu.VMEM((3,) + a_shape, F32),
             pltpu.VMEM((3,) + e_shape, F32),
             pltpu.VMEM((256, 256), BF16),
-            pltpu.SemaphoreType.DMA((steps,)),
             pltpu.SemaphoreType.DMA((2 * steps + 6,)),
-            pltpu.SemaphoreType.DMA((8,)),
         ],
-        compiler_params=pltpu.CompilerParams(vmem_limit_bytes=63 * 1024 * 1024),
-    )(full.reshape(4, 16, 3, 8, PART), g, f, *[v.reshape(a_shape) for v in attn_state], *exp_state)
+        compiler_params=pltpu.CompilerParams(vmem_limit_bytes=16 * 1024 * 1024),
+    )(full_a.reshape(steps, 16, 2, 8, SUB), full_e.reshape(steps // 2, 16, 8, PART), g, f, *[v.reshape(a_shape) for v in attn_state], *exp_state)
     attn_new = [v.reshape(1, width) for v in outs[:3]]
     exp_new = [
         v.reshape(2 * ROWS, 2, LANES).transpose(1, 0, 2).reshape(1, 2, width) for v in outs[3:6]

time: 78.5 us -> 74.1 us (0.944)
  Pallas kernels: 77.8 us -> 73.2 us
    pallas_call x1, Pallas kernels: 5.27 us -> 2.43 us  [body(): pl.pallas_call(finish_kernel, out_shape=(*[jax.ShapeDtypeStruct(a_shape,...]
    pallas_call x1, Pallas kernels: 72.5 us -> 70.8 us  [comm_part(): pl.pallas_call(lambda *refs: comm_kernel(limit, *refs), out_shape=(jax.Sh...]
where the time goes in v4:
time: 74.1 us; the launch traced here: 74 us
  Pallas kernels  73.2 us (99%)
    pallas_call x1, Pallas kernels, comm_part(): pl.pallas_call(lambda *refs: comm_kernel(limit, *refs), out_shape=(jax.Sh...  70.8 us
    pallas_call x1, Pallas kernels, body(): pl.pallas_call(finish_kernel, out_shape=(*[jax.ShapeDtypeStruct(a_shape,...  2.43 us

profile of v4, /device:TPU:1, one launch (start us, length us, event | category | flops | bytes accessed | tf_op | source)
XLA Modules:
  0.0 74.0 jit_solution(13348052944443421885)
XLA Ops:
  0.6 0.0 copy-start.5
  0.6 0.0 copy-start.4
  0.7 0.0 copy-start.3
  0.7 0.0 copy-start.2
  0.7 0.0 copy-start.1
  0.7 0.0 copy-start
  0.7 70.8 %shard_map.161 = (f32[3,48,128]{2,1,0:T(8,128)S(1)}, f32[8,128]{1,0:T(8,128)S(1)}, bf16[2,4,4,4,2,8,768]{6,5,4,3,2,1,0:T(8,128)(2,1)S(1)}, bf16[2,2,4,4,8,1536]{5,4,3,2,1,0:T(8,128)(2,1)S(1)}) custom-call(bf16[256,256]{1,0:T(8,128)(2,1)} %refs_0_.1, bf16[256,6144]{1,0:T(8,128)(2,1)} %refs_1_.1, bf16[1,128,128]{2,1,0:T(8,128)(2,1)} %refs_2_.1, ...), custom_call_target="tpu_custom_call" | custom-call | tf_op jit(solution)/shard_map/pallas_call | solution.py:484
  71.5 0.0 copy-done.5
  71.5 0.0 copy-done.4
  71.5 0.0 copy-done.3
  71.6 0.0 copy-done.2
  71.6 0.0 copy-done.1
  71.6 0.0 copy-done
  71.6 2.4 %shard_map.162 = (f32[48,128]{1,0:T(8,128)}, f32[48,128]{1,0:T(8,128)}, f32[48,128]{1,0:T(8,128)}, f32[96,128]{1,0:T(8,128)}, f32[96,128]{1,0:T(8,128)}, /*index...) custom-call(bf16[8,16,2,8,768]{4,3,2,1,0:T(8,128)(2,1)S(1)} %bitcast.42, ...), custom_call_target="tpu_custom_call" | custom-call | tf_op jit(solution)/shard_map/pallas_call | solution.py:546
Async XLA Ops:
  0.6 70.9 %copy-start.5 = (f32[1,6144]{1,0:T(1,128)S(1)}, f32[1,6144]{1,0:T(1,128)}, u32[]{:S(2)}) copy-start(f32[1,6144]{1,0:T(1,128)} %param.16) | copy-start | bytes 73732
  0.6 70.9 %copy-start.4 = (f32[1,6144]{1,0:T(1,128)S(1)}, f32[1,6144]{1,0:T(1,128)}, u32[]{:S(2)}) copy-start(f32[1,6144]{1,0:T(1,128)} %param.15) | copy-start | bytes 73732
  0.7 70.9 %copy-start.3 = (f32[1,6144]{1,0:T(1,128)S(1)}, f32[1,6144]{1,0:T(1,128)}, u32[]{:S(2)}) copy-start(f32[1,6144]{1,0:T(1,128)} %param.14) | copy-start | bytes 73732
  0.7 70.9 %copy-start.2 = (f32[1,2,6144]{2,1,0:T(2,128)S(1)}, f32[1,2,6144]{2,1,0:T(2,128)}, u32[]{:S(2)}) copy-start(f32[1,2,6144]{2,1,0:T(2,128)} %param.19) | copy-start | bytes 147460
  0.7 70.9 %copy-start.1 = (f32[1,2,6144]{2,1,0:T(2,128)S(1)}, f32[1,2,6144]{2,1,0:T(2,128)}, u32[]{:S(2)}) copy-start(f32[1,2,6144]{2,1,0:T(2,128)} %param.18) | copy-start | bytes 147460
  0.7 70.9 %copy-start = (f32[1,2,6144]{2,1,0:T(2,128)S(1)}, f32[1,2,6144]{2,1,0:T(2,128)}, u32[]{:S(2)}) copy-start(f32[1,2,6144]{2,1,0:T(2,128)} %param.17) | copy-start | bytes 147460

commit v5 on v4

--- a/solution.py
+++ b/solution.py
@@ -45,7 +45,7 @@
 
 
 def device_at(z, y, x, core):
-    return (lax.rem(z, 4), ((y * 4 + x) * 2 + lax.div(z, 4)) * 2 + core)
+    return (z & 3, y * 16 + x * 4 + (z >> 2) * 2 + core)
 
 
 def aligned(index, multiple):
@@ -66,21 +66,26 @@
 ):
     z_lo = lax.axis_index("expert")
     dp = lax.axis_index("dp")
-    core = lax.rem(dp, 2)
-    z_hi = lax.rem(lax.div(dp, 2), 2)
-    x = lax.rem(lax.div(dp, 4), 4)
-    y = lax.div(dp, 16)
+    core = dp & 1
+    z_hi = (dp >> 1) & 1
+    x = (dp >> 2) & 3
+    y = dp >> 4
     z = z_hi * 4 + z_lo
     other = 1 - core
     peer = device_at(z, y, x, other)
 
-    def zc_mate(dz, dc):
-        oz = lax.rem(z + dz, 8)
-        oc = core if dc == 0 else other
-        return oz, oc
+    zc_places, zc_devices, plane_devices = {}, {}, {}
+    for dz in range(8):
+        for dc in range(2):
+            oz, oc = (z + dz) & 7, core if dc == 0 else other
+            zc_places[dz, dc] = (oz, oc)
+            zc_devices[dz, dc] = device_at(oz, y, x, oc)
+    for dy in range(4):
+        for dx in range(4):
+            plane_devices[dy, dx] = device_at(z, (y + dy) & 3, (x + dx) & 3, core)
 
     def plane_mate(dy, dx):
-        return device_at(z, lax.rem(y + dy, 4), lax.rem(x + dx, 4), core)
+        return plane_devices[dy, dx]
 
     def axis_mate(axis, d):
         return plane_mate(d, 0) if axis == 0 else plane_mate(0, d)
@@ -127,6 +132,20 @@
             copy.wait_send()
 
     need_act = (keep(act_a_hbm, act_a), keep(act_e_hbm.at[0], act_e))
+    barrier = pltpu.get_barrier_semaphore()
+    greeted = 0
+    for dz in range(8):
+        for dc in range(2):
+            if dz or dc:
+                oz, oc = zc_places[dz, dc]
+                pl.semaphore_signal(barrier, inc=1, device_id=zc_devices[dz, dc], device_id_type=MESH)
+                greeted += 1
+    for dy in range(4):
+        for dx in range(4):
+            if dy or dx:
+                pl.semaphore_signal(barrier, inc=1, device_id=plane_mate(dy, dx), device_id_type=MESH)
+                greeted += 1
+
     need_dy = {}
     for half in range(2):
         for s in range(4):
@@ -138,20 +157,6 @@
     need_state = [
         keep(src, st_a.at[:, pl.ds(k * ROWS, ROWS)]) for k, src in enumerate((w_a_hbm, m_a_hbm, v_a_hbm))
     ] + [keep(src, dst) for src, dst in ((w_e_hbm, w_e), (m_e_hbm, m_e), (v_e_hbm, v_e))]
-
-    barrier = pltpu.get_barrier_semaphore()
-    greeted = 0
-    for dz in range(8):
-        for dc in range(2):
-            if dz or dc:
-                oz, oc = zc_mate(dz, dc)
-                pl.semaphore_signal(barrier, inc=1, device_id=device_at(oz, y, x, oc), device_id_type=MESH)
-                greeted += 1
-    for dy in range(4):
-        for dx in range(4):
-            if dy or dx:
-                pl.semaphore_signal(barrier, inc=1, device_id=plane_mate(dy, dx), device_id_type=MESH)
-                greeted += 1
 
     r0 = lax.broadcasted_iota(jnp.int32, (256, 256), 0)
     r1_ = lax.broadcasted_iota(jnp.int32, (256, 256), 1)
@@ -201,15 +206,15 @@
         if s < 2:
             copies_1[s] = []
             for e in (2, 1, 3):
-                to = lax.rem(place[first] + e, 4)
+                to = ((place[first] + e) & 3)
                 src = s1.at[s, :, to] if s % 2 == 0 else s1.at[s, to]
                 copies_1[s].append(send(src, r1.at[s, e - 1], axis_mate(first, e)))
         else:
             for d in order:
-                at = lax.rem(place[s % 2] + d, 4)
+                at = ((place[s % 2] + d) & 3)
                 copies_1[s, d] = [
                     send(
-                        piece(s1, s, at, lax.rem(place[first] + e, 4)),
+                        piece(s1, s, at, ((place[first] + e) & 3)),
                         r1.at[s, e - 1, at],
                         axis_mate(first, e),
                     )
@@ -231,10 +236,10 @@
     for dz in z_order:
         for dc in range(2):
             if dz or dc:
-                oz, oc = zc_mate(dz, dc)
-                copies_pf.append(send(st_a.at[oc], pf_a.at[pf_at_a], device_at(oz, y, x, oc)))
+                oz, oc = zc_places[dz, dc]
+                copies_pf.append(send(st_a.at[oc], pf_a.at[pf_at_a], zc_devices[dz, dc]))
                 if dz in (0, 4):
-                    copies_pf.append(send(st_e.at[oc], pf_e.at[pf_at_e], device_at(oz, y, x, oc)))
+                    copies_pf.append(send(st_e.at[oc], pf_e.at[pf_at_e], zc_devices[dz, dc]))
     pf_a[pf_at_a, :] = st_a[core]
     pf_e[pf_at_e, :] = st_e[core]
 
@@ -249,7 +254,7 @@
     copies_2 = {s: [] for s in range(4)}
 
     def pass_on(s, d):
-        at = lax.rem(place[s % 2] + d, 4)
+        at = ((place[s % 2] + d) & 3)
         total = piece(own, s, at, place[1 - s % 2])[...]
         for e in range(3):
             total = total + r1[s, e, at].astype(F32)
@@ -286,12 +291,12 @@
     for dz in z_order:
         for dc in range(2):
             if dz or dc:
-                oz, oc = zc_mate(dz, dc)
-                q = lax.rem(oz, 4) * 4 + lax.div(oz, 4) * 2 + oc
-                batch.append(send(z3_a.at[q], r3_a.at[dc, dz], device_at(oz, y, x, oc)))
+                oz, oc = zc_places[dz, dc]
+                q = (oz & 3) * 4 + (oz >> 2) * 2 + oc
+                batch.append(send(z3_a.at[q], r3_a.at[dc, dz], zc_devices[dz, dc]))
                 if dz in (0, 4):
-                    q = lax.div(oz, 4) * 2 + oc
-                    batch.append(send(z3_e.at[q], r3_e.at[dc, dz // 4], device_at(oz, y, x, oc)))
+                    q = (oz >> 2) * 2 + oc
+                    batch.append(send(z3_e.at[q], r3_e.at[dc, dz // 4], zc_devices[dz, dc]))
     arrive(batch)
 
     near = s3_a[pl.ds(aligned(my_q * ROWS, 8), ROWS), :]
@@ -319,8 +324,8 @@
     for dz in z_order:
         for dc in range(2):
             if dz or dc:
-                oz, oc = zc_mate(dz, dc)
-                batch.append(send(n_s.at[0], n_r.at[0, dz * 2 + dc], device_at(oz, y, x, oc)))
+                oz, oc = zc_places[dz, dc]
+                batch.append(send(n_s.at[0], n_r.at[0, dz * 2 + dc], zc_devices[dz, dc]))
     ws_a[core] = near.astype(BF16)
     ws_a[other] = far.astype(BF16)
     ws_e[core] = near_e.astype(BF16)
@@ -329,10 +334,10 @@
     for dz in z_order:
         for dc in range(2):
             if dz or dc:
-                oz, oc = zc_mate(dz, dc)
-                copies_g.append(send(ws_a.at[oc], gr_a.at[my_q], device_at(oz, y, x, oc)))
+                oz, oc = zc_places[dz, dc]
+                copies_g.append(send(ws_a.at[oc], gr_a.at[my_q], zc_devices[dz, dc]))
                 if dz in (0, 4):
-                    copies_g.append(send(ws_e.at[oc], gr_e.at[my_e], device_at(oz, y, x, oc)))
+                    copies_g.append(send(ws_e.at[oc], gr_e.at[my_e], zc_devices[dz, dc]))
     gr_a[my_q] = ws_a[core]
     gr_e[my_e] = ws_e[core]
     arrive(batch)
@@ -359,11 +364,11 @@
         values = [state[pl.ds(k * ROWS + t, rows, stride=3 * ROWS), :] for k in range(3)]
         return adamw(grad[pl.ds(t, rows, stride=ROWS), :], *values, factor)[0].astype(BF16)
 
-    even = 2 * lax.rem(lax.div(z_lo + 1, 2), 2)
-    odd = 2 * lax.div(z_lo, 2) + 1
+    even = ((z_lo + 1) & 2)
+    odd = (z_lo & 2) + 1
     mine = (even, odd)
     swapped = (2 - even, 4 - odd)
-    swap_z = (lax.rem(z + 1 + 6 * lax.rem(z, 2), 8), lax.rem(z + 7 - 6 * lax.rem(z, 2), 8))
+    swap_z = (z + 1 - 2 * (z & 1), (z + 7 + 2 * (z & 1)) & 7)
 
     def spread(ref, lead, part, at):
         here = block(ref, lead, part, at, place[1 - part])
@@ -396,34 +401,54 @@
         here = gt_e.at[part, y, x]
         for d in (2, 1, 3):
             second_e[part, d] = send(here, here, axis_mate(part, d))
-        first_e[part, 0] = spread(gt_e, part, part, place[part])
 
     def from_mate(part, d):
-        return lax.rem(place[part] + 4 - d, 4)
+        return ((place[part] + 4 - d) & 3)
 
     for d in (1, 3, 2):
         for part in range(2):
             arrive([second_a[part, d]])
             first_a[part, d] = spread(gt_a, mine[part], part, from_mate(part, d))
-    for d in (1, 3, 2):
-        for part in range(2):
-            arrive([second_e[part, d]])
-            first_e[part, d] = spread(gt_e, part, part, from_mate(part, d))
+    for part in range(2):
+        arrive([second_e[part, d] for d in (1, 3, 2)])
+        for e in (2, 1, 3):
+            here = gt_e.at[0, :, x] if part == 0 else gt_e.at[1, y]
+            first_e[part, e] = send(here, here, axis_mate(1 - part, e))
     swaps = {}
-    for d in (0, 1, 3, 2):
+
+    def pass_attention(d):
         for part in range(2):
             at = from_mate(part, d)
             arrive(first_a[part, d])
             ready = strip(gt_a, mine[part], part, at)
             swaps[part, d] = send(ready, ready, device_at(swap_z[part], y, x, core))
             deliver(gt_a, mine[part], part, at)
-    for d in (0, 1, 3, 2):
+
+    def end_expert(e):
         for part in range(2):
-            at = from_mate(part, d)
-            arrive(first_e[part, d])
-            deliver(gt_e, part, part, at)
+            if e:
+                arrive([first_e[part, e]])
+            at = (place[1 - part] + 4 - e) & 3
+            src = gt_e.at[0, :, at] if part == 0 else gt_e.at[1, at]
+            send(src, src, peer)
+
+    def end_swap(d):
+        for part in range(2):
             arrive([swaps[part, d]])
-            deliver(gt_a, swapped[part], part, at)
+            deliver(gt_a, swapped[part], part, from_mate(part, d))
+
+    pass_attention(0)
+    pass_attention(1)
+    end_expert(0)
+    pass_attention(3)
+    end_swap(0)
+    pass_attention(2)
+    end_expert(1)
+    end_swap(1)
+    end_expert(3)
+    end_swap(3)
+    end_expert(2)
+    end_swap(2)
     finish_all()
 
 

time: 74.1 us -> 73.5 us (level)
  no operation moved by 1% of the time
where the time goes in v5:
time: 73.5 us; the launch traced here: 73.4 us
  Pallas kernels  72.6 us (99%)
  between operations  0.74 us (1%)
    pallas_call x1, Pallas kernels, comm_part(): pl.pallas_call(lambda *refs: comm_kernel(limit, *refs), out_shape=(jax.Sh...  70.2 us
    pallas_call x1, Pallas kernels, body(): pl.pallas_call(finish_kernel, out_shape=(*[jax.ShapeDtypeStruct(a_shape,...  2.43 us

profile of v5, /device:TPU:1, one launch (start us, length us, event | category | flops | bytes accessed | tf_op | source)
XLA Modules:
  0.0 73.4 jit_solution(157989336688579884)
XLA Ops:
  0.6 0.0 copy-start.5
  0.6 0.0 copy-start.4
  0.7 0.0 copy-start.3
  0.7 0.0 copy-start.2
  0.7 0.0 copy-start.1
  0.7 0.0 copy-start
  0.7 70.2 %shard_map.161 = (f32[3,48,128]{2,1,0:T(8,128)S(1)}, f32[8,128]{1,0:T(8,128)S(1)}, bf16[2,4,4,4,2,8,768]{6,5,4,3,2,1,0:T(8,128)(2,1)S(1)}, bf16[2,2,4,4,8,1536]{5,4,3,2,1,0:T(8,128)(2,1)S(1)}) custom-call(bf16[256,256]{1,0:T(8,128)(2,1)} %refs_0_.1, bf16[256,6144]{1,0:T(8,128)(2,1)} %refs_1_.1, bf16[1,128,128]{2,1,0:T(8,128)(2,1)} %refs_2_.1, ...), custom_call_target="tpu_custom_call" | custom-call | tf_op jit(solution)/shard_map/pallas_call | solution.py:509
  70.9 0.0 copy-done.5
  70.9 0.0 copy-done.4
  70.9 0.0 copy-done.3
  70.9 0.0 copy-done.2
  70.9 0.0 copy-done.1
  71.0 0.0 copy-done
  71.0 2.4 %shard_map.162 = (f32[48,128]{1,0:T(8,128)}, f32[48,128]{1,0:T(8,128)}, f32[48,128]{1,0:T(8,128)}, f32[96,128]{1,0:T(8,128)}, f32[96,128]{1,0:T(8,128)}, /*index...) custom-call(bf16[8,16,2,8,768]{4,3,2,1,0:T(8,128)(2,1)S(1)} %bitcast.42, ...), custom_call_target="tpu_custom_call" | custom-call | tf_op jit(solution)/shard_map/pallas_call | solution.py:571
Async XLA Ops:
  0.6 70.3 %copy-start.5 = (f32[1,6144]{1,0:T(1,128)S(1)}, f32[1,6144]{1,0:T(1,128)}, u32[]{:S(2)}) copy-start(f32[1,6144]{1,0:T(1,128)} %param.16) | copy-start | bytes 73732
  0.6 70.3 %copy-start.4 = (f32[1,6144]{1,0:T(1,128)S(1)}, f32[1,6144]{1,0:T(1,128)}, u32[]{:S(2)}) copy-start(f32[1,6144]{1,0:T(1,128)} %param.15) | copy-start | bytes 73732
  0.7 70.3 %copy-start.3 = (f32[1,6144]{1,0:T(1,128)S(1)}, f32[1,6144]{1,0:T(1,128)}, u32[]{:S(2)}) copy-start(f32[1,6144]{1,0:T(1,128)} %param.14) | copy-start | bytes 73732
  0.7 70.3 %copy-start.2 = (f32[1,2,6144]{2,1,0:T(2,128)S(1)}, f32[1,2,6144]{2,1,0:T(2,128)}, u32[]{:S(2)}) copy-start(f32[1,2,6144]{2,1,0:T(2,128)} %param.19) | copy-start | bytes 147460
  0.7 70.3 %copy-start.1 = (f32[1,2,6144]{2,1,0:T(2,128)S(1)}, f32[1,2,6144]{2,1,0:T(2,128)}, u32[]{:S(2)}) copy-start(f32[1,2,6144]{2,1,0:T(2,128)} %param.18) | copy-start | bytes 147460
  0.7 70.3 %copy-start = (f32[1,2,6144]{2,1,0:T(2,128)S(1)}, f32[1,2,6144]{2,1,0:T(2,128)}, u32[]{:S(2)}) copy-start(f32[1,2,6144]{2,1,0:T(2,128)} %param.17) | copy-start | bytes 147460

commit v6 on v5

--- a/solution.py
+++ b/solution.py
@@ -203,7 +203,7 @@
             own[s, b] = both
             s1[s, b] = both.astype(BF16)
         first = 1 - s % 2
-        if s < 2:
+        if s < 3:
             copies_1[s] = []
             for e in (2, 1, 3):
                 to = ((place[first] + e) & 3)
@@ -264,12 +264,12 @@
         else:
             own2[s] = total
 
-    for s in (0, 1):
+    for s in (0, 1, 2):
         arrive(copies_1[s])
         for d in order:
             pass_on(s, d)
     for d in order:
-        for s in (2, 3):
+        for s in (3,):
             arrive(copies_1[s, d])
             pass_on(s, d)
 

time: 73.5 us -> 73.9 us (level)
  no operation moved by 1% of the time
where the time goes in v6:
time: 73.9 us; the launch traced here: 73.8 us
  Pallas kernels  73 us (99%)
  between operations  0.74 us (1%)
    pallas_call x1, Pallas kernels, comm_part(): pl.pallas_call(lambda *refs: comm_kernel(limit, *refs), out_shape=(jax.Sh...  70.6 us
    pallas_call x1, Pallas kernels, body(): pl.pallas_call(finish_kernel, out_shape=(*[jax.ShapeDtypeStruct(a_shape,...  2.43 us

profile of v6, /device:TPU:1, one launch (start us, length us, event | category | flops | bytes accessed | tf_op | source)
XLA Modules:
  0.0 73.8 jit_solution(15456781632712827939)
XLA Ops:
  0.6 0.0 copy-start.5
  0.6 0.0 copy-start.4
  0.7 0.0 copy-start.3
  0.7 0.0 copy-start.2
  0.7 0.0 copy-start.1
  0.7 0.0 copy-start
  0.7 70.6 %shard_map.161 = (f32[3,48,128]{2,1,0:T(8,128)S(1)}, f32[8,128]{1,0:T(8,128)S(1)}, bf16[2,4,4,4,2,8,768]{6,5,4,3,2,1,0:T(8,128)(2,1)S(1)}, bf16[2,2,4,4,8,1536]{5,4,3,2,1,0:T(8,128)(2,1)S(1)}) custom-call(bf16[256,256]{1,0:T(8,128)(2,1)} %refs_0_.1, bf16[256,6144]{1,0:T(8,128)(2,1)} %refs_1_.1, bf16[1,128,128]{2,1,0:T(8,128)(2,1)} %refs_2_.1, ...), custom_call_target="tpu_custom_call" | custom-call | tf_op jit(solution)/shard_map/pallas_call | solution.py:509
  71.3 0.0 copy-done.5
  71.3 0.0 copy-done.4
  71.3 0.0 copy-done.3
  71.3 0.0 copy-done.2
  71.3 0.0 copy-done.1
  71.4 0.0 copy-done
  71.4 2.4 %shard_map.162 = (f32[48,128]{1,0:T(8,128)}, f32[48,128]{1,0:T(8,128)}, f32[48,128]{1,0:T(8,128)}, f32[96,128]{1,0:T(8,128)}, f32[96,128]{1,0:T(8,128)}, /*index...) custom-call(bf16[8,16,2,8,768]{4,3,2,1,0:T(8,128)(2,1)S(1)} %bitcast.42, ...), custom_call_target="tpu_custom_call" | custom-call | tf_op jit(solution)/shard_map/pallas_call | solution.py:571
Async XLA Ops:
  0.6 70.7 %copy-start.5 = (f32[1,6144]{1,0:T(1,128)S(1)}, f32[1,6144]{1,0:T(1,128)}, u32[]{:S(2)}) copy-start(f32[1,6144]{1,0:T(1,128)} %param.16) | copy-start | bytes 73732
  0.6 70.7 %copy-start.4 = (f32[1,6144]{1,0:T(1,128)S(1)}, f32[1,6144]{1,0:T(1,128)}, u32[]{:S(2)}) copy-start(f32[1,6144]{1,0:T(1,128)} %param.15) | copy-start | bytes 73732
  0.7 70.7 %copy-start.3 = (f32[1,6144]{1,0:T(1,128)S(1)}, f32[1,6144]{1,0:T(1,128)}, u32[]{:S(2)}) copy-start(f32[1,6144]{1,0:T(1,128)} %param.14) | copy-start | bytes 73732
  0.7 70.7 %copy-start.2 = (f32[1,2,6144]{2,1,0:T(2,128)S(1)}, f32[1,2,6144]{2,1,0:T(2,128)}, u32[]{:S(2)}) copy-start(f32[1,2,6144]{2,1,0:T(2,128)} %param.19) | copy-start | bytes 147460
  0.7 70.7 %copy-start.1 = (f32[1,2,6144]{2,1,0:T(2,128)S(1)}, f32[1,2,6144]{2,1,0:T(2,128)}, u32[]{:S(2)}) copy-start(f32[1,2,6144]{2,1,0:T(2,128)} %param.18) | copy-start | bytes 147460
  0.7 70.7 %copy-start = (f32[1,2,6144]{2,1,0:T(2,128)S(1)}, f32[1,2,6144]{2,1,0:T(2,128)}, u32[]{:S(2)}) copy-start(f32[1,2,6144]{2,1,0:T(2,128)} %param.17) | copy-start | bytes 147460
